TPU v7x, 128 devices: a whole 4x4x4 slice. The times are simulated.
128 devices in a mesh: fsdp: 16 (over z, x_lo, core), rows: 8 (over y, x_hi).
Axes of the slice: x: 4 (x_hi: 2, x_lo: 2; x = x_hi * 2 + x_lo), y: 4, z: 4, core: 2. Of those that a mesh axis runs over, the one named last changes fastest.
Arguments:
- query_rows: bfloat16 [16, 2048, 1536], P('fsdp', 'rows'), may hold values from -6 to 6
- key_rows: bfloat16 [16, 2048, 1536], P('fsdp', 'rows'), may hold values from -6 to 6
- value_rows: bfloat16 [16, 2048, 1536], P('fsdp', 'rows'), may hold values from -6 to 6
- grad_out: bfloat16 [16, 2048, 3072], P('fsdp', 'rows'), may hold values from -6 to 6
- w_out: bfloat16 [1536, 3072], P('fsdp'), may hold values from -0.15625 to 0.15625
Outputs:
- grad_query: bfloat16 [16, 2048, 1536], P('fsdp', 'rows')
- grad_key: bfloat16 [16, 2048, 1536], P('fsdp', 'rows')
- grad_value: bfloat16 [16, 2048, 1536], P('fsdp', 'rows')
- grad_w_out: float32 [1536, 3072], P('fsdp')
All inputs are finite; a program needn't handle non-finite values.
Results may differ from a plain program's by a relative error of at most 0.02.
Values may be sent and summed in bfloat16 or wider, within the bound.
A program may use at most 192 MiB of HBM per device.

v0:
```python
import math

import jax
import jax.numpy as jnp
from jax import lax
from jax.sharding import PartitionSpec as P

HDIM = 128
HEADS = 12
HW = 1536


def in_one_piece(arrays, axis, dim, along):
    both = jnp.concatenate(arrays, axis=along)
    result, at, outs = (lax.all_gather(both, axis, axis=dim, tiled=True), 0, [])
    for a in arrays:
        outs.append(lax.slice_in_dim(result, at, at + a.shape[along], axis=along))
        at += a.shape[along]
    return tuple(outs)


def cut_along(array, dim, devices):
    shape = array.shape
    tiles = array.reshape(*shape[:dim], devices, shape[dim] // devices, *shape[dim + 1 :])
    return jnp.moveaxis(tiles, dim, 0)


def sent_and_summed(array, axis, dim):
    devices = lax.axis_size(axis)
    tiles = lax.all_to_all(cut_along(array, dim, devices), axis, 0, 0, tiled=True)
    return jnp.sum(tiles.astype(jnp.float32), axis=0)


def in_one_piece_2(arrays, axis, dim, along):
    ends, at = ([], 0)
    for a in arrays[:-1]:
        at += a.shape[along]
        ends.append(at)
    both = jnp.concatenate(arrays, axis=along)
    return tuple(jnp.split(sent_and_summed(both, axis, dim), ends, axis=along))


def split_heads(array, count, groups):
    per_group = HEADS // groups
    return jnp.moveaxis(array.reshape(count, groups, per_group, HDIM), 1, 0)


def join_heads(array, count):
    return jnp.moveaxis(array, 0, 1).reshape(count, HW)


def local(query_rows, key_rows, value_rows, grad_out, w_out):
    tokens = query_rows.shape[1]
    factor = 1.0 / math.sqrt(HDIM)
    grad_flat = grad_out[0]
    groups = HEADS // 4
    grad_attn = lax.dot_general(
        grad_flat,
        lax.all_gather(w_out, "fsdp", axis=0, tiled=True),
        (((1,), (1,)), ((), ())),
        preferred_element_type=jnp.float32,
    ).astype(jnp.bfloat16)
    all_keys, all_values = in_one_piece((key_rows, value_rows), "rows", 1, 0)
    length = all_keys.shape[1]

    def attend(inputs):
        query_heads, key_heads, value_heads, grad_heads = inputs
        scores = (
            jnp.einsum("qhd,khd->hqk", query_heads, key_heads, preferred_element_type=jnp.float32)
            * factor
        )
        probs = jax.nn.softmax(scores, axis=-1)
        probs_low = probs.astype(jnp.bfloat16)
        attended = jnp.einsum(
            "hqk,khd->qhd", probs_low, value_heads, preferred_element_type=jnp.float32
        )
        value_part = jnp.einsum(
            "hqk,qhd->khd", probs_low, grad_heads, preferred_element_type=jnp.float32
        )
        grad_probs = jnp.einsum(
            "qhd,khd->hqk", grad_heads, value_heads, preferred_element_type=jnp.float32
        )
        centre = jnp.sum(probs * grad_probs, axis=-1, keepdims=True)
        grad_scores = (probs * (grad_probs - centre)).astype(jnp.bfloat16)
        grad_query = (
            jnp.einsum("hqk,khd->qhd", grad_scores, key_heads, preferred_element_type=jnp.float32)
            * factor
        )
        key_part = (
            jnp.einsum("hqk,qhd->khd", grad_scores, query_heads, preferred_element_type=jnp.float32)
            * factor
        )
        return (
            attended.astype(jnp.bfloat16),
            grad_query.astype(jnp.bfloat16),
            key_part,
            value_part,
        )

    attended, grad_query, key_part, value_part = lax.map(
        attend,
        (
            split_heads(query_rows[0], tokens, groups),
            split_heads(all_keys[0], length, groups),
            split_heads(all_values[0], length, groups),
            split_heads(grad_attn, tokens, groups),
        ),
    )
    attended = join_heads(attended, tokens)
    grad_query = join_heads(grad_query, tokens).reshape(1, tokens, HW)
    key_part = join_heads(key_part, length)
    value_part = join_heads(value_part, length)
    grad_key, grad_value = in_one_piece_2(
        (
            key_part.reshape(1, length, HW).astype(jnp.bfloat16),
            value_part.reshape(1, length, HW).astype(jnp.bfloat16),
        ),
        "rows",
        1,
        0,
    )
    term = lax.dot_general(
        attended, grad_flat, (((0,), (0,)), ((), ())), preferred_element_type=jnp.float32
    )
    partial_grad = sent_and_summed(
        lax.optimization_barrier(term.astype(jnp.bfloat16))
        .astype(jnp.float32)
        .astype(jnp.bfloat16),
        "fsdp",
        0,
    )
    grad_w_out = lax.psum(partial_grad.astype(jnp.bfloat16), "rows").astype(jnp.float32)
    return (grad_query, grad_key.astype(jnp.bfloat16), grad_value.astype(jnp.bfloat16), grad_w_out)


def solution(mesh):
    in_specs = (
        P("fsdp", "rows", None),
        P("fsdp", "rows", None),
        P("fsdp", "rows", None),
        P("fsdp", "rows", None),
        P("fsdp", None),
    )
    out_specs = (
        P("fsdp", "rows", None),
        P("fsdp", "rows", None),
        P("fsdp", "rows", None),
        P("fsdp", None),
    )
    return jax.shard_map(local, mesh=mesh, in_specs=in_specs, out_specs=out_specs, check_vma=False)
```

profile of v0, /device:TPU:16, one launch (start us, length us, event | category | flops | bytes accessed | tf_op | source)
XLA Modules:
  0.0 662.8 jit_solution(4083551851996054782)
XLA Ops:
  13.6 55.5 %all-gather.5.cloned.1.call-done = bf16[1536,3072]{1,0:T(8,128)(2,1)} async-done(((bf16[96,3072]{1,0:T(8,128)(2,1)}), bf16[1536,3072]{1,0:T(8,128)(2,1)}) %all-gather.5.cloned.1.call-update) | async-done | bytes 9437200 | tf_op jit(solution)/shard_map/all_gather | solution.py:59
  69.1 7.2 %convolution_convert_fusion.1 = bf16[256,1536]{1,0:T(8,128)(2,1)} fusion(bf16[1536,3072]{1,0:T(8,128)(2,1)} %all-gather.5.cloned.1.call-done, bf16[1,256,3072]{2,1,0:T(8,128)(2,1)S(1)} %copy-done), kind=kOutput, calls=%fused_computation.48 | convolution fusion | flops 2416312320 | bytes 11796480 | tf_op jit(solution)/shard_map/dot_general | solution.py:57
  79.0 144.8 %all-gather.3.cloned.1.call-done = bf16[2,2048,1536]{1,2,0:T(8,128)(2,1)} async-done(((bf16[2,256,1536]{1,2,0:T(8,128)(2,1)}), bf16[2,2048,1536]{1,2,0:T(8,128)(2,1)}) %all-gather.3.cloned.1.call-update) | async-done | bytes 12582928 | tf_op jit(solution)/shard_map/all_gather | solution.py:15
  223.8 10.6 %fusion.72 = (bf16[1,2048,1536]{1,2,0:T(8,128)(2,1)}, bf16[1,2048,1536]{1,2,0:T(8,128)(2,1)}) fusion(bf16[2,2048,1536]{1,2,0:T(8,128)(2,1)} %all-gather.3.cloned.1.call-done), kind=kLoop, calls=%fused_computation.54 | loop fusion | bytes 25165824 | tf_op jit(solution)/shard_map/slice | solution.py:17
  234.5 125.0 %while.16 = (s32[]{:T(128)}, bf16[3,256,4,128]{1,3,2,0:T(8,128)(2,1)S(1)}, bf16[3,256,4,128]{1,3,2,0:T(8,128)(2,1)}, bf16[3,2048,4,128]{1,3,2,0:T(8,128)(2,1)}, ...) while((s32[]{:T(128)}, ...), condition=%wide.region_4.5_spmd, body=%wide.region_0.4_spmd.sunk | while | flops 3266714624 | bytes 190351520 | solution.py:100
  234.5 2.9 fusion.106
  237.4 4.6 fusion.107
  243.1 9.1 %fusion.108 = bf16[3,256,4,128]{1,3,2,0:T(8,128)(2,1)S(1)} fusion(bf16[3,256,4,128]{1,3,2,0:T(8,128)(2,1)S(1)} %get-tuple-element.193, s32[]{:T(128)S(6)} %copy.79, bf16[3,2048,4,128]{1,3,2,0:T(8,128)(2,1)} %get-tuple-element.207, f32[4,256]{1,0:T(4,128)S(1)} %get-tuple-element.178, f32[4,256,2048]{2,1,0:T(8,128)} %copy-done.1), kind=kOutput, calls=%fused_computation.30.clone.1 | convolution fusion | flops 547490816 | bytes 19141632 | tf_op jit(solution)/shard_map/while/body/eval_jaxpr/hqk,khd->qhd/dot_general | solution.py:74
  252.2 10.0 %bitcast_dynamic-update-slice_fusion.5 = bf16[3,2048,4,128]{1,3,2,0:T(8,128)(2,1)} fusion(bf16[3,2048,4,128]{1,3,2,0:T(8,128)(2,1)} %get-tuple-element.196, s32[]{:T(128)S(6)} %copy.79, bf16[3,256,4,128]{3,1,2,0:T(8,128)(2,1)} %get-tuple-element.210, f32[4,256]{1,0:T(4,128)S(1)} %get-tuple-element.178, f32[4,256,2048]{2,1,0:T(8,128)} %copy-done.1), kind=kOutput, calls=%fused_computation.6.clone.1 | convolution fusion | flops 547359744 | bytes 21238784 | tf_op jit(solution)/shard_map/while/body/eval_jaxpr/hqk,qhd->khd/dot_general | solution.py:77
  262.3 5.6 multiply_reduce_fusion.3
  270.1 3.8 fusion.109
  279.1 4.6 fusion.107
  284.8 9.1 %fusion.108 = bf16[3,256,4,128]{1,3,2,0:T(8,128)(2,1)S(1)} fusion(bf16[3,256,4,128]{1,3,2,0:T(8,128)(2,1)S(1)} %get-tuple-element.193, s32[]{:T(128)S(6)} %copy.79, bf16[3,2048,4,128]{1,3,2,0:T(8,128)(2,1)} %get-tuple-element.207, f32[4,256]{1,0:T(4,128)S(1)} %get-tuple-element.178, f32[4,256,2048]{2,1,0:T(8,128)} %copy-done.1), kind=kOutput, calls=%fused_computation.30.clone.1 | convolution fusion | flops 547490816 | bytes 19141632 | tf_op jit(solution)/shard_map/while/body/eval_jaxpr/hqk,khd->qhd/dot_general | solution.py:74
  293.9 10.1 %bitcast_dynamic-update-slice_fusion.5 = bf16[3,2048,4,128]{1,3,2,0:T(8,128)(2,1)} fusion(bf16[3,2048,4,128]{1,3,2,0:T(8,128)(2,1)} %get-tuple-element.196, s32[]{:T(128)S(6)} %copy.79, bf16[3,256,4,128]{3,1,2,0:T(8,128)(2,1)} %get-tuple-element.210, f32[4,256]{1,0:T(4,128)S(1)} %get-tuple-element.178, f32[4,256,2048]{2,1,0:T(8,128)} %copy-done.1), kind=kOutput, calls=%fused_computation.6.clone.1 | convolution fusion | flops 547359744 | bytes 21238784 | tf_op jit(solution)/shard_map/while/body/eval_jaxpr/hqk,qhd->khd/dot_general | solution.py:77
  304.0 5.6 multiply_reduce_fusion.3
  311.9 3.8 fusion.109
  320.7 4.6 fusion.107
  326.5 9.1 %fusion.108 = bf16[3,256,4,128]{1,3,2,0:T(8,128)(2,1)S(1)} fusion(bf16[3,256,4,128]{1,3,2,0:T(8,128)(2,1)S(1)} %get-tuple-element.193, s32[]{:T(128)S(6)} %copy.79, bf16[3,2048,4,128]{1,3,2,0:T(8,128)(2,1)} %get-tuple-element.207, f32[4,256]{1,0:T(4,128)S(1)} %get-tuple-element.178, f32[4,256,2048]{2,1,0:T(8,128)} %copy-done.1), kind=kOutput, calls=%fused_computation.30.clone.1 | convolution fusion | flops 547490816 | bytes 19141632 | tf_op jit(solution)/shard_map/while/body/eval_jaxpr/hqk,khd->qhd/dot_general | solution.py:74
  335.6 10.0 %bitcast_dynamic-update-slice_fusion.5 = bf16[3,2048,4,128]{1,3,2,0:T(8,128)(2,1)} fusion(bf16[3,2048,4,128]{1,3,2,0:T(8,128)(2,1)} %get-tuple-element.196, s32[]{:T(128)S(6)} %copy.79, bf16[3,256,4,128]{3,1,2,0:T(8,128)(2,1)} %get-tuple-element.210, f32[4,256]{1,0:T(4,128)S(1)} %get-tuple-element.178, f32[4,256,2048]{2,1,0:T(8,128)} %copy-done.1), kind=kOutput, calls=%fused_computation.6.clone.1 | convolution fusion | flops 547359744 | bytes 21238784 | tf_op jit(solution)/shard_map/while/body/eval_jaxpr/hqk,qhd->khd/dot_general | solution.py:77
  345.6 5.6 multiply_reduce_fusion.3
  353.4 3.8 fusion.109
  359.5 5.1 convolution_convert_fusion
  364.5 4.8 all-to-all-start.1
  369.3 5.5 copy.67
  374.9 5.5 copy.66
  381.6 7.8 %copy.52 = bf16[8,2,256,1536]{2,3,1,0:T(8,128)(2,1)} copy(bf16[8,2,256,1536]{2,0,3,1:T(8,128)(2,1)S(1)} %maximum_bitcast_fusion) | data formatting | bytes 25165824 | tf_op jit(solution)/shard_map/transpose | solution.py:25
  389.4 86.4 %all-to-all-done.1 = bf16[16,96,3072]{2,1,0:T(8,128)(2,1)} async-done(((bf16[16,96,3072]{2,1,0:T(8,128)(2,1)}), bf16[16,96,3072]{2,1,0:T(8,128)(2,1)}, u32[]{:S(2)}, u32[]{:S(2)}) %all-to-all-start.1) | async-done | bytes 9437216 | tf_op jit(solution)/shard_map/all_to_all | solution.py:30
  475.9 7.3 %all-to-all-start = ((bf16[8,2,256,1536]{2,3,1,0:T(8,128)(2,1)}), bf16[8,2,256,1536]{2,3,1,0:T(8,128)(2,1)}, u32[]{:S(2)}, u32[]{:S(2)}) async-start(bf16[8,2,256,1536]{2,3,1,0:T(8,128)(2,1)} %copy.52), calls=%async_computation | async-start | bytes 25165824 | tf_op jit(solution)/shard_map/all_to_all | solution.py:30
  483.2 6.6 reduce_sum.40
  491.0 90.8 %all-reduce.2.cloned.1.call-done = bf16[96,3072]{1,0:T(8,128)(2,1)} async-done(((bf16[96,3072]{1,0:T(8,128)(2,1)}), bf16[96,3072]{1,0:T(8,128)(2,1)}) %all-reduce.2.cloned.1.call-update) | async-done | bytes 589840 | tf_op jit(solution)/shard_map/psum | solution.py:132
  584.0 59.6 %all-to-all-done = bf16[8,2,256,1536]{2,3,1,0:T(8,128)(2,1)} async-done(((bf16[8,2,256,1536]{2,3,1,0:T(8,128)(2,1)}), bf16[8,2,256,1536]{2,3,1,0:T(8,128)(2,1)}, u32[]{:S(2)}, u32[]{:S(2)}) %all-to-all-start) | async-done | bytes 12582944 | tf_op jit(solution)/shard_map/all_to_all | solution.py:30
  643.6 6.8 %reduce.1 = bf16[2,256,1536]{1,2,0:T(8,128)(2,1)S(1)} reduce(bf16[8,2,256,1536]{2,3,1,0:T(8,128)(2,1)} %all-to-all-done, bf16[]{:T(256)} %constant.32.clone.1), dimensions={0}, to_apply=%region_5.6.clone | reduce | flops 5505024 | bytes 14155778 | tf_op jit(solution)/shard_map/reduce_sum | solution.py:31
  (48 shorter events, 42.0 us)
Async XLA Ops:
  7.2 61.9 %copy-start = (bf16[1,256,3072]{2,1,0:T(8,128)(2,1)S(1)}, bf16[1,256,3072]{2,1,0:T(8,128)(2,1)}, u32[]{:S(2)}) copy-start(bf16[1,256,3072]{2,1,0:T(8,128)(2,1)} %param.10) | copy-start | bytes 4718596
  7.2 61.9 %all-gather.5.cloned.1.call-start = ((), (), s32[]{:S(2)}) async-start(), calls=%async_computation.3 | async-start | bytes 10027008 | tf_op jit(solution)/shard_map/all_gather | solution.py:59
  7.9 215.9 %all-gather.3.cloned.1.call-start = ((), (), s32[]{:S(2)}) async-start(), calls=%async_computation.2 | async-start | bytes 14155776 | tf_op jit(solution)/shard_map/all_gather | solution.py:15
  79.0 155.5 %copy-start.3 = (bf16[3,256,4,128]{1,3,2,0:T(8,128)(2,1)S(1)}, bf16[3,256,4,128]{1,3,2,0:T(8,128)(2,1)}, u32[]{:S(2)}) copy-start(bf16[3,256,4,128]{1,3,2,0:T(8,128)(2,1)} %custom-call) | copy-start | bytes 2359300
  237.4 5.8 copy-start.1
  262.3 6.5 copy-start.2
  279.0 5.8 copy-start.1
  304.0 6.5 copy-start.2
  320.7 5.8 copy-start.1
  345.6 6.5 copy-start.2
  364.5 111.4 %all-to-all-start.1 = ((bf16[16,96,3072]{2,1,0:T(8,128)(2,1)}), bf16[16,96,3072]{2,1,0:T(8,128)(2,1)}, u32[]{:S(2)}, u32[]{:S(2)}) async-start(bf16[16,96,3072]{2,1,0:T(8,128)(2,1)} %bitcast.137), calls=%async_computation.1 | async-start | bytes 18874368 | tf_op jit(solution)/shard_map/all_to_all | solution.py:30
  475.9 167.7 %all-to-all-start = ((bf16[8,2,256,1536]{2,3,1,0:T(8,128)(2,1)}), bf16[8,2,256,1536]{2,3,1,0:T(8,128)(2,1)}, u32[]{:S(2)}, u32[]{:S(2)}) async-start(bf16[8,2,256,1536]{2,3,1,0:T(8,128)(2,1)} %copy.52), calls=%async_computation | async-start | bytes 25165824 | tf_op jit(solution)/shard_map/all_to_all | solution.py:30
  483.2 6.6 %copy-start.4 = (bf16[3,256,4,128]{1,3,2,0:T(8,128)(2,1)S(1)}, bf16[3,256,4,128]{1,3,2,0:T(8,128)(2,1)}, u32[]{:S(2)}) copy-start(bf16[3,256,4,128]{1,3,2,0:T(8,128)(2,1)} %get-tuple-element.54) | copy-start | bytes 2359300
  483.2 98.6 %all-reduce.2.cloned.1.call-start = ((), (), s32[]{:S(2)}) async-start(), calls=%async_computation.4 | async-start | bytes 1179648 | tf_op jit(solution)/shard_map/psum | solution.py:132
Sparse Core Ops, SparseCore 0:
  9.7 59.2 all-gather.4
  71.2 152.5 all-gather.2
  490.0 91.8 all-reduce.1
where the time goes:
time: 666 us; the launch traced here: 663 us
  waiting for transfers between devices  438 us (66%)
  matrix products  113 us (17%)
  local copies, waits for them, and re-layouts  49.6 us (7%)
  other arithmetic  36.2 us (5%)
  between operations  13.8 us (2%)
  starting transfers between devices  12.2 us (2%)
    all_to_all x2, waiting for transfers between devices, sent_and_summed(): lax.all_to_all(cut_along(array, dim, devices), axis, 0, 0, tiled=True)  146 us
    all_gather x1, waiting for transfers between devices, in_one_piece(): result, at, outs = (lax.all_gather(both, axis, axis=dim, tiled=True), 0, [])  145 us
    psum x1, waiting for transfers between devices, local(): lax.psum(partial_grad.astype(jnp.bfloat16), 'rows').astype(jnp.float32)  90.8 us
    all_gather x1, waiting for transfers between devices, local(): lax.all_gather(w_out, 'fsdp', axis=0, tiled=True)  55.5 us
    dot_general x3, matrix products, attend(): jnp.einsum('hqk,qhd->khd', probs_low, grad_heads, preferred_element_type=...  30.1 us
    dot_general x3, matrix products, attend(): jnp.einsum('hqk,khd->qhd', probs_low, value_heads, preferred_element_type...  27.3 us
    unnamed x13, local copies, waits for them, and re-layouts  19.9 us
    dot_general x3, matrix products, attend(): jnp.einsum('qhd,khd->hqk', grad_heads, value_heads, preferred_element_typ...  16.8 us
  transfers between devices with their start and end apart: 5, of which 5 were waited for; matrix products, arithmetic and copies ran while one was open for 7% of the time, Pallas kernels for 0%

commit v1 on v0

v1 whole, which is shorter than its diff:
```python
import math

import jax
import jax.numpy as jnp
from jax import lax
from jax.experimental import pallas as pl
from jax.experimental.pallas import tpu as pltpu
from jax.sharding import PartitionSpec as P

F32 = jnp.float32
BF16 = jnp.bfloat16
MESH = pl.DeviceIdType.MESH
D = 3072
HW = 1536
HD = 128
TOK = 256
GW = 384
SEQ = 2048
HALF = 1024
KC = 256
NK = SEQ // KC
SCALE = 1.0 / math.sqrt(HD)
CST = SCALE * math.log2(math.e)


def m128(x):
    return pl.multiple_of(x, 128)


def m256(x):
    return pl.multiple_of(x, 256)


def local_copy(src, dst, sem):
    return pltpu.make_async_copy(src, dst, sem)


def remote(src, dst, send_sem, recv_sem, dev):
    return pltpu.make_async_remote_copy(
        src_ref=src, dst_ref=dst, send_sem=send_sem, recv_sem=recv_sem,
        device_id=dev, device_id_type=MESH,
    )


def landed(ref, sem):
    pltpu.make_async_copy(ref, ref, sem).wait()


def dot(a, b):
    return jnp.dot(a, b, preferred_element_type=F32)


def kernel(
    q_hbm, k_hbm, v_hbm, go_hbm, w_hbm,
    gq_out, gk_out, gv_out, gw_out,
    qbuf, kbuf, vbuf, ktb, vtb, go, wbuf, sbuf, pbuf, gat, att, obuf, linv,
    dkacc, dvacc, termb, rsb, redb, gwb, gqb, pk, xbuf, keep, fin,
    ss1, rs1, ls1, ss2, rs2, ss3, rs3, lsg, ssw1, rsw1, ssw2, rsw2,
    ss5, rs5, ss6, rs6, ss7, rs7, ls7, ss8, rs8, ss9, rs9, ls9,
):
    f = lax.axis_index("fsdp")
    r = lax.axis_index("rows")
    z, xl, c = f // 4, (f // 2) % 2, f % 2
    y, xh = r // 2, r % 2
    j = f % 4

    def dev(z_, xl_, c_, y_, xh_):
        return (z_ * 4 + xl_ * 2 + c_, y_ * 2 + xh_)

    def ydev(y_):
        return dev(z, xl, c, y_, xh)

    partner = dev(z, xl, c, y, 1 - xh)
    ins = (k_hbm, v_hbm, q_hbm)

    def slot(t, hh, ys):
        if t == 2:
            return qbuf.at[hh, pl.ds(m256(ys * TOK), TOK), :]
        return (kbuf, vbuf)[t].at[hh, pl.ds(m256((xh * 4 + ys) * TOK), TOK), :]

    def cols(t, hh, yd):
        return ins[t].at[0, :, pl.ds(m128(yd * GW + hh * HD), HD)]

    w_own = wbuf.at[pl.ds(pl.multiple_of(j * 96, 32), 96), :]

    @pl.when(z == y)
    def _():
        local_copy(w_hbm, w_own, rsw1.at[0]).start()
        for dz in (1, 2, 3):
            remote(w_hbm, w_own, ssw1.at[dz - 1], rsw1.at[0], dev((z + dz) % 4, xl, c, y, xh)).start()

    def send_head(hh, carry):
        for t in range(3):
            for d in (1, 3, 2):
                yd = (y + d) % 4
                i = (hh * 3 + t) * 3 + d - 1
                remote(cols(t, hh, yd), slot(t, hh, y), ss1.at[i], rs1.at[i], ydev(yd)).start()
            local_copy(cols(t, hh, y), slot(t, hh, y), ls1.at[hh * 3 + t]).start()
        return carry

    lax.fori_loop(0, 3, send_head, 0)

    def go_slot(ys, h, n=1):
        return go.at[pl.ds(pl.multiple_of(ys * TOK + h * 128, 128), 128 * n), :]

    def go_src(h):
        return go_hbm.at[0, pl.ds(h * 128, 128), :]

    yr, yl = (y + 1) % 4, (y + 3) % 4
    yo = (y + 2) % 4
    remote(go_src(0), go_slot(y, 0), ss3.at[0], rs3.at[0], ydev(yr)).start()
    remote(go_src(1), go_slot(y, 1), ss3.at[2], rs3.at[2], ydev(yl)).start()
    remote(go_src(1), go_slot(y, 1), ss3.at[1], rs3.at[1], ydev(yr)).start()
    remote(go_src(0), go_slot(y, 0), ss3.at[3], rs3.at[3], ydev(yl)).start()
    local_copy(go_hbm.at[0], go_slot(y, 0, 2), lsg.at[0]).start()

    def kv_half(t, hh, h):
        return (kbuf, vbuf)[t].at[hh, pl.ds(m256(h * HALF), HALF), :]

    def relay(hh, carry):
        for t in range(2):
            local_copy(cols(t, hh, y), slot(t, hh, y), ls1.at[hh * 3 + t]).wait()
            for d in (1, 3, 2):
                i = (hh * 3 + t) * 3 + d - 1
                landed(slot(t, hh, (y + 4 - d) % 4), rs1.at[i])
            i = hh * 2 + t
            half = kv_half(t, hh, xh)
            remote(half, half, ss2.at[i], rs2.at[i], partner).start()
        return carry

    lax.fori_loop(0, 3, relay, 0)

    landed(w_own, rsw1.at[0])
    for n in (1, 2, 3):
        a, b = n // 2, n % 2
        remote(w_own, w_own, ssw2.at[n - 1], rsw2.at[n - 1],
               dev(z, (xl + a) % 2, (c + b) % 2, y, xh)).start()

    def forward(hh, carry):
        for t in range(2):
            landed(kv_half(t, hh, 1 - xh), rs2.at[hh * 2 + t])
        local_copy(cols(2, hh, y), slot(2, hh, y), ls1.at[hh * 3 + 2]).wait()
        for d in (1, 3, 2):
            landed(slot(2, hh, (y + 4 - d) % 4), rs1.at[(hh * 3 + 2) * 3 + d - 1])
        for kc in range(NK):
            ks = slice(kc * KC, (kc + 1) * KC)
            ktb[hh, :, ks] = kbuf[hh, ks, :].T
            vtb[hh, :, ks] = vbuf[hh, ks, :].T

        def block(qb, carry):
            i = hh * 4 + qb
            qs = pl.ds(m256(qb * TOK), TOK)
            qt = qbuf[hh, qs, :].T
            m = jnp.full((1, TOK), -jnp.inf, F32)
            for kc in range(NK):
                ks = slice(kc * KC, (kc + 1) * KC)
                s = dot(kbuf[hh, ks, :], qt)
                sbuf[ks, :] = s
                m = jnp.maximum(m, jnp.max(s, axis=0, keepdims=True))
            mc = m * CST
            l = jnp.zeros((1, TOK), F32)
            o = jnp.zeros((HD, TOK), F32)
            for kc in range(NK):
                ks = slice(kc * KC, (kc + 1) * KC)
                p = jnp.exp2(sbuf[ks, :] * CST - mc)
                l = l + jnp.sum(p, axis=0, keepdims=True)
                pb = p.astype(BF16)
                pbuf[i, ks, :] = pb
                o = o + dot(vtb[hh, :, ks], pb)
            inv = 1.0 / l
            on = o * inv
            obuf[i] = on
            att[pl.ds(m128(hh * HD), HD), qs] = on.astype(BF16)
            linv[i] = jnp.broadcast_to(inv, (8, TOK))
            return carry

        return lax.fori_loop(0, 4, block, carry)

    forward(0, 0)

    landed(go_slot(yl, 0), rs3.at[0])
    remote(go_slot(yl, 0), go_slot(yl, 0), ss3.at[4], rs3.at[4], ydev(yr)).start()
    landed(go_slot(yr, 1), rs3.at[2])
    remote(go_slot(yr, 1), go_slot(yr, 1), ss3.at[5], rs3.at[5], ydev(yl)).start()

    lax.fori_loop(1, 3, forward, 0)

    for n in (1, 2, 3):
        a, b = n // 2, n % 2
        jn = ((xl + a) % 2) * 2 + (c + b) % 2
        landed(wbuf.at[pl.ds(pl.multiple_of(jn * 96, 32), 96), :], rsw2.at[n - 1])

    def project(ys):
        rows = pl.ds(m256(ys * TOK), TOK)
        g = lax.dot_general(wbuf[...], go[rows, :], (((1,), (1,)), ((), ())), preferred_element_type=F32)
        gat[ys] = g.astype(BF16)

    local_copy(go_hbm.at[0], go_slot(y, 0, 2), lsg.at[0]).wait()
    landed(go_slot(yl, 1), rs3.at[1])
    landed(go_slot(yr, 0), rs3.at[3])
    landed(go_slot(yo, 0), rs3.at[4])
    landed(go_slot(yo, 1), rs3.at[5])

    def project_all(d, carry):
        project((y + d) % 4)
        return carry

    lax.fori_loop(0, 4, project_all, 0)

    def term(o, carry):
        zd, xd = (z + o // 2) % 4, (xh + o % 2) % 2
        col = zd * 2 + xd
        cs = pl.ds(m128(col * GW), GW)
        termb[col] = dot(att[...], go[:, cs]).astype(BF16)
        for n in range(4):
            a, b = n // 2, n % 2
            xld, cd = (xl + a) % 2, (c + b) % 2
            jd = xld * 2 + cd
            piece = termb.at[col, pl.ds(pl.multiple_of(jd * 96, 32), 96), :]
            i = o * 4 + n

            def go_out():
                remote(piece, rsb.at[i], ss5.at[i], rs5.at[i], dev(zd, xld, cd, y, xd)).start()

            if n == 0:
                pl.when(o > 0)(go_out)
            else:
                go_out()
        return carry

    lax.fori_loop(0, 8, term, 0)

    def back_slot(out, hh, yd, ysrc):
        del yd
        return out.at[0, :, pl.ds(m128(ysrc * GW + hh * HD), HD)]

    def hand_out(buf, out, hh, ss, rs, ls, base, lbase):
        for d in (1, 3, 2):
            yd = (y + d) % 4
            remote(buf(yd), back_slot(out, hh, yd, y), ss.at[base + d - 1], rs.at[base + d - 1], ydev(yd)).start()
        local_copy(buf(y), back_slot(out, hh, y, y), ls.at[lbase]).start()

    def finish_kv(hh):
        for t in range(2):
            i = hh * 2 + t
            landed(xbuf.at[i], rs8.at[i])
            fin[i] = (keep[i] + xbuf[i].astype(F32)).astype(BF16)
            hand_out(
                lambda yd: fin.at[i, pl.ds(m256(yd * TOK), TOK), :],
                (gk_out, gv_out)[t], hh, ss9, rs9, ls9, i * 3, i,
            )

    def backward(hh, carry):
        dkacc[...] = jnp.zeros_like(dkacc)
        dvacc[...] = jnp.zeros_like(dvacc)

        def block(qb, carry):
            i = hh * 4 + qb
            qs = pl.ds(m256(qb * TOK), TOK)
            qn = qbuf[hh, qs, :]
            inv = linv[i][0:1, :]
            gt = (gat[qb, pl.ds(m128(hh * HD), HD), :].astype(F32) * inv).astype(BF16)
            gn = gt.T
            cen = jnp.sum(gt.astype(F32) * obuf[i], axis=0, keepdims=True)
            dq = jnp.zeros((HD, TOK), F32)
            for kc in range(NK):
                ks = slice(kc * KC, (kc + 1) * KC)
                dp = dot(vbuf[hh, ks, :], gt)
                pb = pbuf[i, ks, :]
                ds = (pb.astype(F32) * (dp - cen)).astype(BF16)
                dq = dq + dot(ktb[hh, :, ks], ds)
                dkacc[ks, :] += dot(ds, qn)
                dvacc[ks, :] += dot(pb, gn)
            gqb[hh, qs, :] = (dq * SCALE).T.astype(BF16)
            return carry

        lax.fori_loop(0, 4, block, 0)
        mine, other = pl.ds(m256(xh * HALF), HALF), pl.ds(m256((1 - xh) * HALF), HALF)
        for t in range(2):
            acc = (dkacc, dvacc)[t]
            fac = (SCALE, 1.0)[t]
            i = hh * 2 + t
            pk[i] = (acc[other, :] * fac).astype(BF16)
            remote(pk.at[i], xbuf.at[i], ss8.at[i], rs8.at[i], partner).start()
            keep[i] = acc[mine, :] * fac
        hand_out(lambda yd: gqb.at[hh, pl.ds(m256(yd * TOK), TOK), :], gq_out, hh, ss7, rs7, ls7, hh * 3, hh)

        @pl.when(hh > 0)
        def _():
            finish_kv(hh - 1)

        return carry

    lax.fori_loop(0, 3, backward, 0)

    own = z * 2 + xh
    acc = termb[own, pl.ds(pl.multiple_of(j * 96, 32), 96), :].astype(F32)

    def add(i, acc):
        landed(rsb.at[i], rs5.at[i])
        return acc + rsb[i].astype(F32)

    redb[...] = lax.fori_loop(1, 32, add, acc).astype(BF16)
    for n in range(8):
        d, e = n // 2, n % 2
        yd, xd = (y + d) % 4, (xh + e) % 2

        def out_remote():
            remote(redb, gwb.at[own], ss6.at[n], rs6.at[own], dev(y, xl, c, yd, xd)).start()

        if n == 0:
            pl.when(z != y)(out_remote)

            @pl.when(z == y)
            def _():
                local_copy(redb, gwb.at[own], rs6.at[own]).start()
        else:
            out_remote()

    finish_kv(2)

    for n in range(8):
        landed(gwb.at[n], rs6.at[n])
        gw_out[:, n * GW : (n + 1) * GW] = gwb[n].astype(F32)

    def collect(hh, carry):
        for d in (1, 2, 3):
            ys = (y + 4 - d) % 4
            landed(back_slot(gq_out, hh, y, ys), rs7.at[hh * 3 + d - 1])
            for t in range(2):
                landed(back_slot((gk_out, gv_out)[t], hh, y, ys), rs9.at[(hh * 2 + t) * 3 + d - 1])
        landed(back_slot(gq_out, hh, y, y), ls7.at[hh])
        for t in range(2):
            landed(back_slot((gk_out, gv_out)[t], hh, y, y), ls9.at[hh * 2 + t])
        return carry

    lax.fori_loop(0, 3, collect, 0)

    @pl.when(z == y)
    def _():
        for n in range(3):
            landed(w_hbm, ssw1.at[n])

    for n in range(3):
        landed(w_own, ssw2.at[n])

    def left_head(hh, carry):
        for t in range(3):
            for d in (1, 2, 3):
                landed(slot(t, hh, y), ss1.at[(hh * 3 + t) * 3 + d - 1])
        for t in range(2):
            i = hh * 2 + t
            landed(kv_half(t, hh, xh), ss2.at[i])
            landed(pk.at[i], ss8.at[i])
            for d in (1, 2, 3):
                landed(fin.at[i, 0:TOK, :], ss9.at[i * 3 + d - 1])
        for d in (1, 2, 3):
            landed(gqb.at[hh, 0:TOK, :], ss7.at[hh * 3 + d - 1])
        return carry

    lax.fori_loop(0, 3, left_head, 0)
    for n in range(6):
        landed(go_slot(y, 0), ss3.at[n])

    def left_term(i, carry):
        landed(rsb.at[i], ss5.at[i])
        return carry

    lax.fori_loop(1, 32, left_term, 0)

    @pl.when(z != y)
    def _():
        landed(redb, ss6.at[0])

    for n in range(1, 8):
        landed(redb, ss6.at[n])


def local(query_rows, key_rows, value_rows, grad_out, w_out):
    any_spec = pl.BlockSpec(memory_space=pl.ANY)
    dma = pltpu.SemaphoreType.DMA
    vm = pltpu.VMEM
    rows = jax.ShapeDtypeStruct((1, TOK, HW), BF16)
    return pl.pallas_call(
        kernel,
        out_shape=(rows, rows, rows, jax.ShapeDtypeStruct((96, D), F32)),
        in_specs=[any_spec] * 5,
        out_specs=(any_spec, any_spec, any_spec, pl.BlockSpec(memory_space=pltpu.VMEM)),
        scratch_shapes=[
            vm((3, HALF, HD), BF16),
            vm((3, SEQ, HD), BF16),
            vm((3, SEQ, HD), BF16),
            vm((3, HD, SEQ), BF16),
            vm((3, HD, SEQ), BF16),
            vm((HALF, D), BF16),
            vm((GW, D), BF16),
            vm((SEQ, TOK), F32),
            vm((12, SEQ, TOK), BF16),
            vm((4, GW, TOK), BF16),
            vm((GW, HALF), BF16),
            vm((12, HD, TOK), F32),
            vm((12, 8, TOK), F32),
            vm((SEQ, HD), F32),
            vm((SEQ, HD), F32),
            vm((8, GW, GW), BF16),
            vm((32, 96, GW), BF16),
            vm((96, GW), BF16),
            vm((8, 96, GW), BF16),
            vm((3, HALF, HD), BF16),
            vm((6, HALF, HD), BF16),
            vm((6, HALF, HD), BF16),
            vm((6, HALF, HD), F32),
            vm((6, HALF, HD), BF16),
            dma((27,)), dma((27,)), dma((9,)),
            dma((6,)), dma((6,)),
            dma((6,)), dma((6,)), dma((1,)),
            dma((3,)), dma((1,)), dma((3,)), dma((3,)),
            dma((32,)), dma((32,)),
            dma((8,)), dma((8,)),
            dma((9,)), dma((9,)), dma((3,)),
            dma((6,)), dma((6,)),
            dma((18,)), dma((18,)), dma((6,)),
        ],
        compiler_params=pltpu.CompilerParams(
            has_side_effects=True, vmem_limit_bytes=60 * 1024 * 1024
        ),
    )(query_rows, key_rows, value_rows, grad_out, w_out)


def solution(mesh):
    in_specs = (
        P("fsdp", "rows", None),
        P("fsdp", "rows", None),
        P("fsdp", "rows", None),
        P("fsdp", "rows", None),
        P("fsdp", None),
    )
    out_specs = (
        P("fsdp", "rows", None),
        P("fsdp", "rows", None),
        P("fsdp", "rows", None),
        P("fsdp", None),
    )
    return jax.shard_map(local, mesh=mesh, in_specs=in_specs, out_specs=out_specs, check_vma=False)
```

time: 666 us -> 192 us (0.29)
  waiting for transfers between devices: 438 us -> 0 us
  Pallas kernels: 0 us -> 181 us
  matrix products: 113 us -> 0 us
  local copies, waits for them, and re-layouts: 49.6 us -> 6.12 us
  other arithmetic: 36.2 us -> 0 us
  between operations: 13.8 us -> 0.65 us
  starting transfers between devices: 12.2 us -> 0 us
    all_gather x2 -> x0, waiting for transfers between devices: 200 us -> none  [the longest x1 145 us: in_one_piece(): result, at, outs = (lax.all_gather(both, axis, axis=dim, tiled=True), 0, [])]
    pallas_call x0 -> x1, Pallas kernels: none -> 181 us  [local(): pl.pallas_call(kernel, out_shape=(rows, rows, rows, jax.ShapeDtypeStruct(...]
    all_to_all x2 -> x0, waiting for transfers between devices: 146 us -> none  [sent_and_summed(): lax.all_to_all(cut_along(array, dim, devices), axis, 0, 0, tiled=True)]
    dot_general x20 -> x0, matrix products: 113 us -> none  [the longest x3 30.1 us: attend(): jnp.einsum('hqk,qhd->khd', probs_low, grad_heads, preferred_element_type=...]
    psum x1 -> x0, waiting for transfers between devices: 90.8 us -> none  [local(): lax.psum(partial_grad.astype(jnp.bfloat16), 'rows').astype(jnp.float32)]
    sub x3 -> x0, other arithmetic: 13.9 us -> none  [attend(): probs = jax.nn.softmax(scores, axis=-1)]
    unnamed x13 -> x10, local copies, waits for them, and re-layouts: 19.9 us -> 6.12 us
    reduce_sum x2 -> x0, other arithmetic: 13.4 us -> none  [sent_and_summed(): return jnp.sum(tiles.astype(jnp.float32), axis=0)]
  transfers between devices with their start and end apart: 5 -> 0, of which waited for: 5 -> 0; matrix products, arithmetic and copies ran while one was open for 7% -> 0% of each run, Pallas kernels for 0% -> 0%
where the time goes in v1:
time: 192 us; the launch traced here: 188 us
  Pallas kernels  181 us (94%)
  local copies, waits for them, and re-layouts  6.12 us (3%)
    pallas_call x1, Pallas kernels, local(): pl.pallas_call(kernel, out_shape=(rows, rows, rows, jax.ShapeDtypeStruct(...  181 us
    unnamed x10, local copies, waits for them, and re-layouts  6.12 us

profile of v1, /device:TPU:16, one launch (start us, length us, event | category | flops | bytes accessed | tf_op | source)
XLA Modules:
  0.0 188.1 jit_solution(8115363901936371769)
XLA Ops:
  0.6 181.4 %shard_map.84 = (bf16[1,256,1536]{2,1,0:T(8,128)(2,1)}, bf16[1,256,1536]{2,1,0:T(8,128)(2,1)}, bf16[1,256,1536]{2,1,0:T(8,128)(2,1)}, f32[96,3072]{1,0:T(8,128)}) custom-call(bf16[1,256,1536]{2,1,0:T(8,128)(2,1)} %q_hbm.1, bf16[1,256,1536]{2,1,0:T(8,128)(2,1)} %k_hbm.1, bf16[1,256,1536]{2,1,0:T(8,128)(2,1)} %v_hbm.1, bf16[1,256,3072]{2,1,0:T(8,128)(2,1)} %go_hbm.1, ...), custom_call_target="tpu_custom_call" | custom-call | tf_op jit(solution)/shard_map/pallas_call | solution.py:384
  182.0 0.0 copy-start.2
  182.0 2.1 %copy.13 = bf16[1,256,1536]{2,1,0:T(8,128)(2,1)} copy(bf16[1,256,1536]{2,1,0:T(8,128)(2,1)} %get-tuple-element.8) | data formatting | bytes 1572864
  184.2 0.0 copy-done.2
  184.2 0.0 copy-start.1
  184.2 0.9 copy.14
  185.0 0.5 copy-done.1
  185.6 0.0 copy-start
  185.6 0.9 copy.15
  186.5 0.7 copy-done
  187.1 1.0 copy.16
Async XLA Ops:
  182.0 2.1 %copy-start.2 = (bf16[1,256,1536]{2,1,0:T(8,128)(2,1)S(1)}, bf16[1,256,1536]{2,1,0:T(8,128)(2,1)}, u32[]{:S(2)}) copy-start(bf16[1,256,1536]{2,1,0:T(8,128)(2,1)} %get-tuple-element.9) | copy-start | bytes 2359300
  184.2 1.4 copy-start.1
  185.6 1.6 copy-start

commit v2 on v1

--- a/solution.py
+++ b/solution.py
@@ -54,9 +54,9 @@
     q_hbm, k_hbm, v_hbm, go_hbm, w_hbm,
     gq_out, gk_out, gv_out, gw_out,
     qbuf, kbuf, vbuf, ktb, vtb, go, wbuf, sbuf, pbuf, gat, att, obuf, linv,
-    dkacc, dvacc, termb, rsb, redb, gwb, gqb, pk, xbuf, keep, fin,
+    dkacc, dvacc, termb, rsb, part, pin, redb, gwb, gqb, pk, xbuf, keep, fin,
     ss1, rs1, ls1, ss2, rs2, ss3, rs3, lsg, ssw1, rsw1, ssw2, rsw2,
-    ss5, rs5, ss6, rs6, ss7, rs7, ls7, ss8, rs8, ss9, rs9, ls9,
+    ss5, rs5, ss6, rs6, ss7, rs7, ls7, ss8, rs8, ss9, rs9, ls9, ss10, rs10,
 ):
     f = lax.axis_index("fsdp")
     r = lax.axis_index("rows")
@@ -81,7 +81,10 @@
     def cols(t, hh, yd):
         return ins[t].at[0, :, pl.ds(m128(yd * GW + hh * HD), HD)]
 
-    w_own = wbuf.at[pl.ds(pl.multiple_of(j * 96, 32), 96), :]
+    def w_rows(n):
+        return wbuf.at[pl.ds(pl.multiple_of(n * 96, 32), 96), :]
+
+    w_own = w_rows(j)
 
     @pl.when(z == y)
     def _():
@@ -131,10 +134,8 @@
     lax.fori_loop(0, 3, relay, 0)
 
     landed(w_own, rsw1.at[0])
-    for n in (1, 2, 3):
-        a, b = n // 2, n % 2
-        remote(w_own, w_own, ssw2.at[n - 1], rsw2.at[n - 1],
-               dev(z, (xl + a) % 2, (c + b) % 2, y, xh)).start()
+    remote(w_own, w_own, ssw2.at[0], rsw2.at[0], dev(z, xl, 1 - c, y, xh)).start()
+    remote(w_own, w_own, ssw2.at[1], rsw2.at[1], dev(z, 1 - xl, c, y, xh)).start()
 
     def forward(hh, carry):
         for t in range(2):
@@ -177,6 +178,9 @@
         return lax.fori_loop(0, 4, block, carry)
 
     forward(0, 0)
+    w_across = w_rows((1 - xl) * 2 + c)
+    landed(w_across, rsw2.at[1])
+    remote(w_across, w_across, ssw2.at[2], rsw2.at[2], dev(z, xl, 1 - c, y, xh)).start()
 
     landed(go_slot(yl, 0), rs3.at[0])
     remote(go_slot(yl, 0), go_slot(yl, 0), ss3.at[4], rs3.at[4], ydev(yr)).start()
@@ -185,10 +189,8 @@
 
     lax.fori_loop(1, 3, forward, 0)
 
-    for n in (1, 2, 3):
-        a, b = n // 2, n % 2
-        jn = ((xl + a) % 2) * 2 + (c + b) % 2
-        landed(wbuf.at[pl.ds(pl.multiple_of(jn * 96, 32), 96), :], rsw2.at[n - 1])
+    landed(w_rows(xl * 2 + 1 - c), rsw2.at[0])
+    landed(w_rows((1 - xl) * 2 + 1 - c), rsw2.at[2])
 
     def project(ys):
         rows = pl.ds(m256(ys * TOK), TOK)
@@ -208,27 +210,44 @@
     lax.fori_loop(0, 4, project_all, 0)
 
     def term(o, carry):
-        zd, xd = (z + o // 2) % 4, (xh + o % 2) % 2
-        col = zd * 2 + xd
-        cs = pl.ds(m128(col * GW), GW)
-        termb[col] = dot(att[...], go[:, cs]).astype(BF16)
-        for n in range(4):
-            a, b = n // 2, n % 2
-            xld, cd = (xl + a) % 2, (c + b) % 2
-            jd = xld * 2 + cd
-            piece = termb.at[col, pl.ds(pl.multiple_of(jd * 96, 32), 96), :]
-            i = o * 4 + n
+        zd = (z + 1 + o) % 4
+        for xd in range(2):
+            cs = pl.ds(m128((zd * 2 + xd) * GW), GW)
+            t = dot(att[...], go[:, cs]).astype(BF16)
+            for n in range(4):
+                termb[zd, n % 2, xd, n // 2] = t[n * 96 : (n + 1) * 96, :]
+        for b in range(2):
+            i = o * 2 + b
+            cd = (c + b) % 2
 
             def go_out():
-                remote(piece, rsb.at[i], ss5.at[i], rs5.at[i], dev(zd, xld, cd, y, xd)).start()
-
-            if n == 0:
-                pl.when(o > 0)(go_out)
+                remote(termb.at[zd, cd], rsb.at[i], ss5.at[i], rs5.at[i], dev(zd, xl, cd, y, xh)).start()
+
+            if b == 0:
+                pl.when(o < 3)(go_out)
             else:
                 go_out()
         return carry
 
-    lax.fori_loop(0, 8, term, 0)
+    lax.fori_loop(0, 4, term, 0)
+
+    def reduce_planes():
+        def add(i, carry):
+            landed(rsb.at[i], rs5.at[i])
+            return carry
+
+        lax.fori_loop(0, 6, add, 0)
+        landed(rsb.at[7], rs5.at[7])
+        for e in range(2):
+            for a in range(2):
+                t = termb[z, c, e, a].astype(F32) + rsb[7, e, a].astype(F32)
+                for i in range(6):
+                    t = t + rsb[i, e, a].astype(F32)
+                part[e, a] = t.astype(BF16)
+        for n in (1, 2, 3):
+            a, e = n // 2, n % 2
+            xld, xhd = (xl + a) % 2, (xh + e) % 2
+            remote(part.at[xhd, xld], pin.at[n], ss10.at[n], rs10.at[n], dev(z, xld, c, y, xhd)).start()
 
     def back_slot(out, hh, yd, ysrc):
         del yd
@@ -289,18 +308,20 @@
         def _():
             finish_kv(hh - 1)
 
+        @pl.when(hh == 2)
+        def _():
+            reduce_planes()
+
         return carry
 
     lax.fori_loop(0, 3, backward, 0)
 
     own = z * 2 + xh
-    acc = termb[own, pl.ds(pl.multiple_of(j * 96, 32), 96), :].astype(F32)
-
-    def add(i, acc):
-        landed(rsb.at[i], rs5.at[i])
-        return acc + rsb[i].astype(F32)
-
-    redb[...] = lax.fori_loop(1, 32, add, acc).astype(BF16)
+    acc = part[xh, xl].astype(F32)
+    for n in (1, 2, 3):
+        landed(pin.at[n], rs10.at[n])
+        acc = acc + pin[n].astype(F32)
+    redb[...] = acc.astype(BF16)
     for n in range(8):
         d, e = n // 2, n % 2
         yd, xd = (y + d) % 4, (xh + e) % 2
@@ -362,11 +383,10 @@
     for n in range(6):
         landed(go_slot(y, 0), ss3.at[n])
 
-    def left_term(i, carry):
-        landed(rsb.at[i], ss5.at[i])
-        return carry
-
-    lax.fori_loop(1, 32, left_term, 0)
+    for n in (0, 1, 2, 3, 4, 5, 7):
+        landed(rsb.at[n], ss5.at[n])
+    for n in (1, 2, 3):
+        landed(redb, ss10.at[n])
 
     @pl.when(z != y)
     def _():
@@ -402,8 +422,10 @@
             vm((12, 8, TOK), F32),
             vm((SEQ, HD), F32),
             vm((SEQ, HD), F32),
-            vm((8, GW, GW), BF16),
-            vm((32, 96, GW), BF16),
+            vm((4, 2, 2, 2, 96, GW), BF16),
+            vm((8, 2, 2, 96, GW), BF16),
+            vm((2, 2, 96, GW), BF16),
+            vm((4, 96, GW), BF16),
             vm((96, GW), BF16),
             vm((8, 96, GW), BF16),
             vm((3, HALF, HD), BF16),
@@ -415,11 +437,12 @@
             dma((6,)), dma((6,)),
             dma((6,)), dma((6,)), dma((1,)),
             dma((3,)), dma((1,)), dma((3,)), dma((3,)),
-            dma((32,)), dma((32,)),
+            dma((8,)), dma((8,)),
             dma((8,)), dma((8,)),
             dma((9,)), dma((9,)), dma((3,)),
             dma((6,)), dma((6,)),
             dma((18,)), dma((18,)), dma((6,)),
+            dma((4,)), dma((4,)),
         ],
         compiler_params=pltpu.CompilerParams(
             has_side_effects=True, vmem_limit_bytes=60 * 1024 * 1024

time: 192 us -> 171 us (0.89)
  Pallas kernels: 181 us -> 162 us
    pallas_call x1, Pallas kernels: 181 us -> 162 us  [local(): pl.pallas_call(kernel, out_shape=(rows, rows, rows, jax.ShapeDtypeStruct(...]
where the time goes in v2:
time: 171 us; the launch traced here: 168 us
  Pallas kernels  162 us (95%)
  local copies, waits for them, and re-layouts  6.12 us (4%)
    pallas_call x1, Pallas kernels, local(): pl.pallas_call(kernel, out_shape=(rows, rows, rows, jax.ShapeDtypeStruct(...  162 us
    unnamed x10, local copies, waits for them, and re-layouts  6.12 us

profile of v2, /device:TPU:16, one launch (start us, length us, event | category | flops | bytes accessed | tf_op | source)
XLA Modules:
  0.0 168.4 jit_solution(9618065361168630158)
XLA Ops:
  0.6 161.6 %shard_map.84 = (bf16[1,256,1536]{2,1,0:T(8,128)(2,1)}, bf16[1,256,1536]{2,1,0:T(8,128)(2,1)}, bf16[1,256,1536]{2,1,0:T(8,128)(2,1)}, f32[96,3072]{1,0:T(8,128)}) custom-call(bf16[1,256,1536]{2,1,0:T(8,128)(2,1)} %q_hbm.1, bf16[1,256,1536]{2,1,0:T(8,128)(2,1)} %k_hbm.1, bf16[1,256,1536]{2,1,0:T(8,128)(2,1)} %v_hbm.1, bf16[1,256,3072]{2,1,0:T(8,128)(2,1)} %go_hbm.1, ...), custom_call_target="tpu_custom_call" | custom-call | tf_op jit(solution)/shard_map/pallas_call | solution.py:404
  162.2 0.0 copy-start.2
  162.2 2.1 %copy.13 = bf16[1,256,1536]{2,1,0:T(8,128)(2,1)} copy(bf16[1,256,1536]{2,1,0:T(8,128)(2,1)} %get-tuple-element.8) | data formatting | bytes 1572864
  164.4 0.0 copy-done.2
  164.4 0.0 copy-start.1
  164.4 0.9 copy.14
  165.3 0.5 copy-done.1
  165.8 0.0 copy-start
  165.8 0.9 copy.15
  166.7 0.7 copy-done
  167.3 1.0 copy.16
Async XLA Ops:
  162.2 2.1 %copy-start.2 = (bf16[1,256,1536]{2,1,0:T(8,128)(2,1)S(1)}, bf16[1,256,1536]{2,1,0:T(8,128)(2,1)}, u32[]{:S(2)}) copy-start(bf16[1,256,1536]{2,1,0:T(8,128)(2,1)} %get-tuple-element.9) | copy-start | bytes 2359300
  164.4 1.4 copy-start.1
  165.8 1.6 copy-start

commit v3 on v2

v3 whole, which is shorter than its diff:
```python
import math

import jax
import jax.numpy as jnp
from jax import lax
from jax.experimental import pallas as pl
from jax.experimental.pallas import tpu as pltpu
from jax.sharding import PartitionSpec as P

F32 = jnp.float32
BF16 = jnp.bfloat16
MESH = pl.DeviceIdType.MESH
D = 3072
HW = 1536
HD = 128
TOK = 256
GW = 384
HALF = 1024
KC = 256
NK = HALF // KC
SCALE = 1.0 / math.sqrt(HD)
CST = SCALE * math.log2(math.e)


def m128(x):
    return pl.multiple_of(x, 128)


def m256(x):
    return pl.multiple_of(x, 256)


def local_copy(src, dst, sem):
    return pltpu.make_async_copy(src, dst, sem)


def remote(src, dst, send_sem, recv_sem, dev):
    return pltpu.make_async_remote_copy(
        src_ref=src, dst_ref=dst, send_sem=send_sem, recv_sem=recv_sem,
        device_id=dev, device_id_type=MESH,
    )


def landed(ref, sem):
    pltpu.make_async_copy(ref, ref, sem).wait()


def dot(a, b):
    return jnp.dot(a, b, preferred_element_type=F32)


def kernel(
    q_hbm, k_hbm, v_hbm, go_hbm, w_hbm,
    gq_out, gk_out, gv_out, gw_out,
    qbuf, kbuf, vbuf, ktb, vtb, go, wbuf, sbuf, pbuf, att, obuf, stat, rbuf,
    oxs, oxr, sxs, sxr, g1, c1, gxs, gxr, cxs, cxr, dqk, dqxs, dqxr, finq,
    dkacc, dvacc, fin, termb, cin, zsum, zin, part, pin, redb, gwb,
    ss1, rs1, ls1, ss2, rs2, ss3, rs3, lsg, ssw1, rsw1, ssw2, rsw2,
    ss4, rs4, ss5, rs5, ss6, rs6, ss7, rs7, ls7, ss8, rs8, ss9, rs9, ls9,
    ss10, rs10, ss11, rs11, ss12, rs12,
):
    f = lax.axis_index("fsdp")
    r = lax.axis_index("rows")
    z, xl, c = f // 4, (f // 2) % 2, f % 2
    y, xh = r // 2, r % 2
    j = f % 4

    def dev(z_, xl_, c_, y_, xh_):
        return (z_ * 4 + xl_ * 2 + c_, y_ * 2 + xh_)

    def ydev(y_):
        return dev(z, xl, c, y_, xh)

    partner = dev(z, xl, c, y, 1 - xh)
    coremate = dev(z, xl, 1 - c, y, xh)
    ins = (k_hbm, v_hbm, q_hbm)

    def slot(t, hh, ys):
        if t == 2:
            return qbuf.at[hh, pl.ds(m256((xh * 4 + ys) * TOK), TOK), :]
        return (kbuf, vbuf)[t].at[hh, pl.ds(m256(ys * TOK), TOK), :]

    def cols(t, hh, yd):
        return ins[t].at[0, :, pl.ds(m128(yd * GW + hh * HD), HD)]

    def w_rows(n):
        return wbuf.at[pl.ds(pl.multiple_of(n * 96, 32), 96), :]

    w_own = w_rows(j)

    @pl.when(z == y)
    def _():
        local_copy(w_hbm, w_own, rsw1.at[0]).start()
        for dz in (1, 2, 3):
            remote(w_hbm, w_own, ssw1.at[dz - 1], rsw1.at[0], dev((z + dz) % 4, xl, c, y, xh)).start()

    def send_head(hh, carry):
        for t in (2, 0, 1):
            for d in (1, 3, 2):
                yd = (y + d) % 4
                i = (hh * 3 + t) * 3 + d - 1
                remote(cols(t, hh, yd), slot(t, hh, y), ss1.at[i], rs1.at[i], ydev(yd)).start()
            local_copy(cols(t, hh, y), slot(t, hh, y), ls1.at[hh * 3 + t]).start()
        return carry

    lax.fori_loop(0, 3, send_head, 0)

    def go_slot(ys, h, n=1):
        return go.at[pl.ds(pl.multiple_of(ys * TOK + h * 128, 128), 128 * n), :]

    def go_src(h):
        return go_hbm.at[0, pl.ds(h * 128, 128), :]

    yr, yl = (y + 1) % 4, (y + 3) % 4
    yo = (y + 2) % 4
    remote(go_src(0), go_slot(y, 0), ss3.at[0], rs3.at[0], ydev(yr)).start()
    remote(go_src(1), go_slot(y, 1), ss3.at[2], rs3.at[2], ydev(yl)).start()
    remote(go_src(1), go_slot(y, 1), ss3.at[1], rs3.at[1], ydev(yr)).start()
    remote(go_src(0), go_slot(y, 0), ss3.at[3], rs3.at[3], ydev(yl)).start()
    local_copy(go_hbm.at[0], go_slot(y, 0, 2), lsg.at[0]).start()

    def arrived(t, hh):
        local_copy(cols(t, hh, y), slot(t, hh, y), ls1.at[hh * 3 + t]).wait()
        for d in (1, 3, 2):
            landed(slot(t, hh, (y + 4 - d) % 4), rs1.at[(hh * 3 + t) * 3 + d - 1])

    def q_half(hh, h):
        return qbuf.at[hh, pl.ds(pl.multiple_of(h * HALF, HALF), HALF), :]

    def relay(hh, carry):
        arrived(2, hh)
        remote(q_half(hh, xh), q_half(hh, xh), ss2.at[hh], rs2.at[hh], partner).start()
        return carry

    lax.fori_loop(0, 3, relay, 0)

    landed(w_own, rsw1.at[0])
    remote(w_own, w_own, ssw2.at[0], rsw2.at[0], coremate).start()
    remote(w_own, w_own, ssw2.at[1], rsw2.at[1], dev(z, 1 - xl, c, y, xh)).start()

    def scores_block(hh, s):
        i = hh * 8 + s
        qt = qbuf[hh, pl.ds(m256(s * TOK), TOK), :].T
        m = jnp.full((1, TOK), -jnp.inf, F32)
        for kc in range(NK):
            ks = slice(kc * KC, (kc + 1) * KC)
            sc = dot(kbuf[hh, ks, :], qt)
            sbuf[ks, :] = sc
            m = jnp.maximum(m, jnp.max(sc, axis=0, keepdims=True))
        mc = m * CST
        l = jnp.zeros((1, TOK), F32)
        o = jnp.zeros((HD, TOK), F32)
        for kc in range(NK):
            ks = slice(kc * KC, (kc + 1) * KC)
            p = jnp.exp2(sbuf[ks, :] * CST - mc)
            l = l + jnp.sum(p, axis=0, keepdims=True)
            pb = p.astype(BF16)
            pbuf[i, ks, :] = pb
            o = o + dot(vtb[hh, :, ks], pb)
        return m, l, o

    def forward(hh, carry):
        arrived(0, hh)
        arrived(1, hh)
        for kc in range(NK):
            ks = slice(kc * KC, (kc + 1) * KC)
            ktb[hh, :, ks] = kbuf[hh, ks, :].T
            vtb[hh, :, ks] = vbuf[hh, ks, :].T
        landed(q_half(hh, 1 - xh), rs2.at[hh])

        def theirs(ys, carry):
            m, l, o = scores_block(hh, (1 - xh) * 4 + ys)
            oxs[hh, ys] = o.astype(BF16)
            sxs[hh, ys, 0:1, :] = m
            sxs[hh, ys, 1:2, :] = l
            return carry

        lax.fori_loop(0, 4, theirs, 0)
        remote(oxs.at[hh], oxr.at[hh], ss4.at[hh], rs4.at[hh], partner).start()
        remote(sxs.at[hh], sxr.at[hh], ss4.at[hh + 3], rs4.at[hh + 3], partner).start()

        def mine(ys, carry):
            m, l, o = scores_block(hh, xh * 4 + ys)
            obuf[hh, ys] = o
            stat[hh, ys, 0:1, :] = m
            stat[hh, ys, 1:2, :] = l
            return carry

        return lax.fori_loop(0, 4, mine, carry)

    lax.fori_loop(0, 3, forward, 0)

    w_across = w_rows((1 - xl) * 2 + c)
    landed(w_across, rsw2.at[1])
    remote(w_across, w_across, ssw2.at[2], rsw2.at[2], coremate).start()

    def merge(hh, carry):
        landed(oxr.at[hh], rs4.at[hh])
        landed(sxr.at[hh], rs4.at[hh + 3])

        def block(ys, carry):
            ma, la = stat[hh, ys, 0:1, :], stat[hh, ys, 1:2, :]
            mb, lb = sxr[hh, ys, 0:1, :], sxr[hh, ys, 1:2, :]
            m = jnp.maximum(ma, mb)
            ea, eb = jnp.exp2((ma - m) * CST), jnp.exp2((mb - m) * CST)
            inv = 1.0 / (la * ea + lb * eb)
            ra, rb = ea * inv, eb * inv
            o = obuf[hh, ys] * ra + oxr[hh, ys].astype(F32) * rb
            obuf[hh, ys] = o
            att[pl.ds(m128(hh * HD), HD), pl.ds(m256(ys * TOK), TOK)] = o.astype(BF16)
            rbuf[hh, ys, 0:1, :] = ra
            rbuf[hh, ys, 1:2, :] = rb
            return carry

        return lax.fori_loop(0, 4, block, carry)

    lax.fori_loop(0, 3, merge, 0)
    landed(w_rows(xl * 2 + 1 - c), rsw2.at[0])
    landed(w_rows((1 - xl) * 2 + 1 - c), rsw2.at[2])

    def project(ys):
        g = lax.dot_general(
            wbuf[...], go[pl.ds(m256(ys * TOK), TOK), :], (((1,), (1,)), ((), ())), preferred_element_type=F32
        )
        for hh in range(3):
            gh = g[hh * HD : (hh + 1) * HD, :]
            cen = jnp.sum(gh * obuf[hh, ys], axis=0, keepdims=True)
            ra, rb = rbuf[hh, ys, 0:1, :], rbuf[hh, ys, 1:2, :]
            g1[ys, hh] = (gh * ra).astype(BF16)
            gxs[ys, hh] = (gh * rb).astype(BF16)
            c1[ys, hh, 0:1, :] = cen * ra
            cxs[ys, hh, 0:1, :] = cen * rb
        remote(gxs.at[ys], gxr.at[ys], ss8.at[ys], rs8.at[ys], partner).start()
        remote(cxs.at[ys], cxr.at[ys], ss8.at[ys + 4], rs8.at[ys + 4], partner).start()

    dkacc[...] = jnp.zeros_like(dkacc)
    dvacc[...] = jnp.zeros_like(dvacc)

    def backward(own, ys, after=None):
        s = (xh if own else 1 - xh) * 4 + ys

        def head(hh, carry):
            i = hh * 8 + s
            qn = qbuf[hh, pl.ds(m256(s * TOK), TOK), :]
            gt = (g1 if own else gxr)[ys, hh]
            cen = (c1 if own else cxr)[ys, hh, 0:1, :]
            gn = gt.T
            dq = jnp.zeros((HD, TOK), F32)
            for kc in range(NK):
                ks = slice(kc * KC, (kc + 1) * KC)
                dp = dot(vbuf[hh, ks, :], gt)
                pb = pbuf[i, ks, :]
                ds = (pb.astype(F32) * (dp - cen)).astype(BF16)
                dq = dq + dot(ktb[hh, :, ks], ds)
                dkacc[hh, ks, :] += dot(ds, qn)
                dvacc[hh, ks, :] += dot(pb, gn)
            dqn = (dq * SCALE).T
            hs = pl.ds(m128(hh * HD), HD)
            if own:
                dqk[ys, :, hs] = dqn
            else:
                dqxs[ys, :, hs] = dqn.astype(BF16)
            if after is not None:
                after(hh)
            return carry

        lax.fori_loop(0, 3, head, 0)

    def theirs_in(ys):
        landed(gxr.at[ys], rs8.at[ys])
        landed(cxr.at[ys], rs8.at[ys + 4])

    def send_dq(ys):
        remote(dqxs.at[ys], dqxr.at[ys], ss12.at[ys], rs12.at[ys], partner).start()

    def q_cols(ysrc):
        return gq_out.at[0, :, pl.ds(m128(ysrc * GW), GW)]

    def finish_q(d):
        ys = (y + d) % 4
        landed(dqxr.at[ys], rs12.at[ys])
        finq[ys] = (dqk[ys] + dqxr[ys].astype(F32)).astype(BF16)
        if d == 0:
            local_copy(finq.at[ys], q_cols(y), ls7.at[0]).start()
        else:
            remote(finq.at[ys], q_cols(y), ss7.at[d - 1], rs7.at[d - 1], ydev(ys)).start()

    local_copy(go_hbm.at[0], go_slot(y, 0, 2), lsg.at[0]).wait()
    project(y)
    backward(True, y)

    landed(go_slot(yl, 0), rs3.at[0])
    remote(go_slot(yl, 0), go_slot(yl, 0), ss3.at[4], rs3.at[4], ydev(yr)).start()
    landed(go_slot(yr, 1), rs3.at[2])
    remote(go_slot(yr, 1), go_slot(yr, 1), ss3.at[5], rs3.at[5], ydev(yl)).start()

    theirs_in(y)
    backward(False, y)
    send_dq(y)

    landed(go_slot(yl, 1), rs3.at[1])
    project(yl)
    finish_q(0)
    backward(True, yl)
    landed(go_slot(yr, 0), rs3.at[3])
    project(yr)
    theirs_in(yl)
    backward(False, yl)
    send_dq(yl)
    backward(True, yr)
    theirs_in(yr)
    backward(False, yr)
    send_dq(yr)
    finish_q(3)

    landed(go_slot(yo, 0), rs3.at[4])
    landed(go_slot(yo, 1), rs3.at[5])
    project(yo)

    def term(o, carry):
        zd = (z + 1 + o) % 4
        for xd in range(2):
            cs = pl.ds(m128((zd * 2 + xd) * GW), GW)
            t = dot(att[...], go[:, cs]).astype(BF16)
            for n in range(4):
                termb[zd, n % 2, xd, n // 2] = t[n * 96 : (n + 1) * 96, :]
        remote(termb.at[zd, 1 - c], cin.at[zd], ss5.at[zd], rs5.at[zd], coremate).start()
        return carry

    lax.fori_loop(0, 4, term, 0)
    backward(True, yo)

    def to_z(o, carry):
        zd = (z + 1 + o) % 4
        landed(cin.at[zd], rs5.at[zd])
        for e in range(2):
            for a in range(2):
                t = termb[zd, c, e, a].astype(F32) + cin[zd, e, a].astype(F32)
                zsum[o, e, a] = t.astype(BF16)

        @pl.when(o < 3)
        def _():
            remote(zsum.at[o], zin.at[o], ss11.at[o], rs11.at[o], dev(zd, xl, c, y, xh)).start()

        return carry

    lax.fori_loop(0, 4, to_z, 0)
    finish_q(1)

    def back_slot(out, hh, ysrc):
        return out.at[0, :, pl.ds(m128(ysrc * GW + hh * HD), HD)]

    def hand_out(hh):
        for t in range(2):
            i = hh * 2 + t
            fin[i] = ((dkacc, dvacc)[t][hh] * (SCALE, 1.0)[t]).astype(BF16)
            out = (gk_out, gv_out)[t]
            for d in (1, 3, 2):
                yd = (y + d) % 4
                n = i * 3 + d - 1
                remote(fin.at[i, pl.ds(m256(yd * TOK), TOK), :], back_slot(out, hh, y), ss9.at[n], rs9.at[n],
                       ydev(yd)).start()
            local_copy(fin.at[i, pl.ds(m256(y * TOK), TOK), :], back_slot(out, hh, y), ls9.at[i]).start()

    theirs_in(yo)
    backward(False, yo, hand_out)
    send_dq(yo)

    for i in range(3):
        landed(zin.at[i], rs11.at[i])
    for e in range(2):
        for a in range(2):
            t = zsum[3, e, a].astype(F32)
            for i in range(3):
                t = t + zin[i, e, a].astype(F32)
            part[e, a] = t.astype(BF16)
    for n in (1, 2, 3):
        a, e = n // 2, n % 2
        xld, xhd = (xl + a) % 2, (xh + e) % 2
        remote(part.at[xhd, xld], pin.at[n], ss10.at[n], rs10.at[n], dev(z, xld, c, y, xhd)).start()
    finish_q(2)

    own = z * 2 + xh
    acc = part[xh, xl].astype(F32)
    for n in (1, 2, 3):
        landed(pin.at[n], rs10.at[n])
        acc = acc + pin[n].astype(F32)
    redb[...] = acc.astype(BF16)
    for n in range(8):
        d, e = n // 2, n % 2
        yd, xd = (y + d) % 4, (xh + e) % 2

        def out_remote():
            remote(redb, gwb.at[own], ss6.at[n], rs6.at[own], dev(y, xl, c, yd, xd)).start()

        if n == 0:
            pl.when(z != y)(out_remote)

            @pl.when(z == y)
            def _():
                local_copy(redb, gwb.at[own], rs6.at[own]).start()
        else:
            out_remote()

    landed(q_cols(y), ls7.at[0])
    for d in (1, 2, 3):
        landed(q_cols((y + 4 - d) % 4), rs7.at[d - 1])

    def collect(hh, carry):
        for t in range(2):
            i = hh * 2 + t
            out = (gk_out, gv_out)[t]
            for d in (1, 2, 3):
                landed(back_slot(out, hh, (y + 4 - d) % 4), rs9.at[i * 3 + d - 1])
            landed(back_slot(out, hh, y), ls9.at[i])
        return carry

    lax.fori_loop(0, 3, collect, 0)
    for n in range(8):
        landed(gwb.at[n], rs6.at[n])
        gw_out[:, n * GW : (n + 1) * GW] = gwb[n].astype(F32)

    @pl.when(z == y)
    def _():
        for n in range(3):
            landed(w_hbm, ssw1.at[n])

    for n in range(3):
        landed(w_own, ssw2.at[n])

    def left_head(hh, carry):
        for t in range(3):
            for d in (1, 2, 3):
                landed(slot(t, hh, y), ss1.at[(hh * 3 + t) * 3 + d - 1])
        landed(q_half(hh, xh), ss2.at[hh])
        landed(oxs.at[hh], ss4.at[hh])
        landed(sxs.at[hh], ss4.at[hh + 3])
        for t in range(2):
            for d in (1, 2, 3):
                landed(fin.at[hh, 0:TOK, :], ss9.at[(hh * 2 + t) * 3 + d - 1])
        return carry

    lax.fori_loop(0, 3, left_head, 0)
    for n in range(6):
        landed(go_slot(y, 0), ss3.at[n])
    for n in range(4):
        landed(gxs.at[n], ss8.at[n])
        landed(cxs.at[n], ss8.at[n + 4])
        landed(dqxs.at[n], ss12.at[n])
        landed(cin.at[n], ss5.at[n])
    for n in range(3):
        landed(finq.at[n], ss7.at[n])
        landed(zin.at[n], ss11.at[n])
        landed(redb, ss10.at[n + 1])

    @pl.when(z != y)
    def _():
        landed(redb, ss6.at[0])

    for n in range(1, 8):
        landed(redb, ss6.at[n])


def local(query_rows, key_rows, value_rows, grad_out, w_out):
    any_spec = pl.BlockSpec(memory_space=pl.ANY)
    dma = pltpu.SemaphoreType.DMA
    vm = pltpu.VMEM
    rows = jax.ShapeDtypeStruct((1, TOK, HW), BF16)
    return pl.pallas_call(
        kernel,
        out_shape=(rows, rows, rows, jax.ShapeDtypeStruct((96, D), F32)),
        in_specs=[any_spec] * 5,
        out_specs=(any_spec, any_spec, any_spec, pl.BlockSpec(memory_space=pltpu.VMEM)),
        scratch_shapes=[
            vm((3, 2 * HALF, HD), BF16),
            vm((3, HALF, HD), BF16),
            vm((3, HALF, HD), BF16),
            vm((3, HD, HALF), BF16),
            vm((3, HD, HALF), BF16),
            vm((HALF, D), BF16),
            vm((GW, D), BF16),
            vm((HALF, TOK), F32),
            vm((24, HALF, TOK), BF16),
            vm((GW, HALF), BF16),
            vm((3, 4, HD, TOK), F32),
            vm((3, 4, 8, TOK), F32),
            vm((3, 4, 8, TOK), F32),
            vm((3, 4, HD, TOK), BF16),
            vm((3, 4, HD, TOK), BF16),
            vm((3, 4, 8, TOK), F32),
            vm((3, 4, 8, TOK), F32),
            vm((4, 3, HD, TOK), BF16),
            vm((4, 3, 8, TOK), F32),
            vm((4, 3, HD, TOK), BF16),
            vm((4, 3, HD, TOK), BF16),
            vm((4, 3, 8, TOK), F32),
            vm((4, 3, 8, TOK), F32),
            vm((4, TOK, GW), F32),
            vm((4, TOK, GW), BF16),
            vm((4, TOK, GW), BF16),
            vm((4, TOK, GW), BF16),
            vm((3, HALF, HD), F32),
            vm((3, HALF, HD), F32),
            vm((6, HALF, HD), BF16),
            vm((4, 2, 2, 2, 96, GW), BF16),
            vm((4, 2, 2, 96, GW), BF16),
            vm((4, 2, 2, 96, GW), BF16),
            vm((3, 2, 2, 96, GW), BF16),
            vm((2, 2, 96, GW), BF16),
            vm((4, 96, GW), BF16),
            vm((96, GW), BF16),
            vm((8, 96, GW), BF16),
            dma((27,)), dma((27,)), dma((9,)),
            dma((3,)), dma((3,)),
            dma((6,)), dma((6,)), dma((1,)),
            dma((3,)), dma((1,)), dma((3,)), dma((3,)),
            dma((6,)), dma((6,)),
            dma((4,)), dma((4,)),
            dma((8,)), dma((8,)),
            dma((3,)), dma((3,)), dma((1,)),
            dma((8,)), dma((8,)),
            dma((18,)), dma((18,)), dma((6,)),
            dma((4,)), dma((4,)),
            dma((3,)), dma((3,)),
            dma((4,)), dma((4,)),
        ],
        compiler_params=pltpu.CompilerParams(
            has_side_effects=True, vmem_limit_bytes=60 * 1024 * 1024
        ),
    )(query_rows, key_rows, value_rows, grad_out, w_out)


def solution(mesh):
    in_specs = (
        P("fsdp", "rows", None),
        P("fsdp", "rows", None),
        P("fsdp", "rows", None),
        P("fsdp", "rows", None),
        P("fsdp", None),
    )
    out_specs = (
        P("fsdp", "rows", None),
        P("fsdp", "rows", None),
        P("fsdp", "rows", None),
        P("fsdp", None),
    )
    return jax.shard_map(local, mesh=mesh, in_specs=in_specs, out_specs=out_specs, check_vma=False)
```

time: 171 us -> 158 us (0.924); the launches traced: 168 us -> 157 us
  Pallas kernels: 162 us -> 151 us
    pallas_call x1, Pallas kernels: 162 us -> 151 us  [local(): pl.pallas_call(kernel, out_shape=(rows, rows, rows, jax.ShapeDtypeStruct(...]
where the time goes in v3:
time: 158 us; the launch traced here: 157 us
  Pallas kernels  151 us (96%)
  local copies, waits for them, and re-layouts  6.12 us (4%)
    pallas_call x1, Pallas kernels, local(): pl.pallas_call(kernel, out_shape=(rows, rows, rows, jax.ShapeDtypeStruct(...  151 us
    unnamed x10, local copies, waits for them, and re-layouts  6.12 us

profile of v3, /device:TPU:16, one launch (start us, length us, event | category | flops | bytes accessed | tf_op | source)
XLA Modules:
  0.0 157.4 jit_solution(17148852389511546642)
XLA Ops:
  0.6 150.6 %shard_map.84 = (bf16[1,256,1536]{2,1,0:T(8,128)(2,1)}, bf16[1,256,1536]{2,1,0:T(8,128)(2,1)}, bf16[1,256,1536]{2,1,0:T(8,128)(2,1)}, f32[96,3072]{1,0:T(8,128)}) custom-call(bf16[1,256,1536]{2,1,0:T(8,128)(2,1)} %q_hbm.1, bf16[1,256,1536]{2,1,0:T(8,128)(2,1)} %k_hbm.1, bf16[1,256,1536]{2,1,0:T(8,128)(2,1)} %v_hbm.1, bf16[1,256,3072]{2,1,0:T(8,128)(2,1)} %go_hbm.1, ...), custom_call_target="tpu_custom_call" | custom-call | tf_op jit(solution)/shard_map/pallas_call | solution.py:469
  151.2 0.0 copy-start.2
  151.2 2.1 %copy.13 = bf16[1,256,1536]{2,1,0:T(8,128)(2,1)} copy(bf16[1,256,1536]{2,1,0:T(8,128)(2,1)} %get-tuple-element.8) | data formatting | bytes 1572864
  153.4 0.0 copy-done.2
  153.4 0.0 copy-start.1
  153.4 0.9 copy.14
  154.3 0.5 copy-done.1
  154.8 0.0 copy-start
  154.8 0.9 copy.15
  155.7 0.7 copy-done
  156.3 1.0 copy.16
Async XLA Ops:
  151.2 2.1 %copy-start.2 = (bf16[1,256,1536]{2,1,0:T(8,128)(2,1)S(1)}, bf16[1,256,1536]{2,1,0:T(8,128)(2,1)}, u32[]{:S(2)}) copy-start(bf16[1,256,1536]{2,1,0:T(8,128)(2,1)} %get-tuple-element.9) | copy-start | bytes 2359300
  153.4 1.4 copy-start.1
  154.8 1.6 copy-start

commit v4 on v3

--- a/solution.py
+++ b/solution.py
@@ -54,10 +54,10 @@
     gq_out, gk_out, gv_out, gw_out,
     qbuf, kbuf, vbuf, ktb, vtb, go, wbuf, sbuf, pbuf, att, obuf, stat, rbuf,
     oxs, oxr, sxs, sxr, g1, c1, gxs, gxr, cxs, cxr, dqk, dqxs, dqxr, finq,
-    dkacc, dvacc, fin, termb, cin, zsum, zin, part, pin, redb, gwb,
+    dkacc, dvacc, fin, termb, cin, zsum, zin, part, pin, gst, tacc,
     ss1, rs1, ls1, ss2, rs2, ss3, rs3, lsg, ssw1, rsw1, ssw2, rsw2,
     ss4, rs4, ss5, rs5, ss6, rs6, ss7, rs7, ls7, ss8, rs8, ss9, rs9, ls9,
-    ss10, rs10, ss11, rs11, ss12, rs12,
+    ss10, rs10, ss11, rs11, ss12, rs12, ss13, rs13, lsw,
 ):
     f = lax.axis_index("fsdp")
     r = lax.axis_index("rows")
@@ -87,6 +87,19 @@
         return wbuf.at[pl.ds(pl.multiple_of(n * 96, 32), 96), :]
 
     w_own = w_rows(j)
+
+    barrier = pltpu.get_barrier_semaphore()
+
+    def hello(d):
+        pl.semaphore_signal(barrier, inc=1, device_id=d, device_id_type=MESH)
+
+    for d in (1, 2, 3):
+        hello(ydev((y + d) % 4))
+        hello(dev(z, xl, c, (y + d) % 4, 1 - xh))
+        hello(dev((z + d) % 4, xl, c, y, xh))
+        hello(dev(z, (xl + d // 2) % 2, c, y, (xh + d % 2) % 2))
+    hello(coremate)
+    pl.semaphore_wait(barrier, 13)
 
     @pl.when(z == y)
     def _():
@@ -298,9 +311,24 @@
     backward(False, y)
     send_dq(y)
 
+    def term_cols(zd, xd):
+        return pl.ds(m128((zd * 2 + xd) * GW), GW)
+
+    def term_dot(ys, zd, xd):
+        at = pl.ds(m256(ys * TOK), TOK)
+        return dot(att[:, at], go[at, term_cols(zd, xd)])
+
+    def term_part(ys, first=False):
+        def add(n, carry):
+            t = term_dot(ys, n // 2, n % 2)
+            tacc[n] = t if first else tacc[n] + t
+            return carry
+
+        lax.fori_loop(0, 8, add, 0)
+
+    term_part(y, True)
     landed(go_slot(yl, 1), rs3.at[1])
     project(yl)
-    finish_q(0)
     backward(True, yl)
     landed(go_slot(yr, 0), rs3.at[3])
     project(yr)
@@ -311,7 +339,9 @@
     theirs_in(yr)
     backward(False, yr)
     send_dq(yr)
-    finish_q(3)
+    term_part(yl)
+    term_part(yr)
+    finish_q(0)
 
     landed(go_slot(yo, 0), rs3.at[4])
     landed(go_slot(yo, 1), rs3.at[5])
@@ -320,14 +350,15 @@
     def term(o, carry):
         zd = (z + 1 + o) % 4
         for xd in range(2):
-            cs = pl.ds(m128((zd * 2 + xd) * GW), GW)
-            t = dot(att[...], go[:, cs]).astype(BF16)
+            t = (tacc[zd * 2 + xd] + term_dot(yo, zd, xd)).astype(BF16)
             for n in range(4):
                 termb[zd, n % 2, xd, n // 2] = t[n * 96 : (n + 1) * 96, :]
         remote(termb.at[zd, 1 - c], cin.at[zd], ss5.at[zd], rs5.at[zd], coremate).start()
         return carry
 
     lax.fori_loop(0, 4, term, 0)
+    finish_q(3)
+    finish_q(1)
     backward(True, yo)
 
     def to_z(o, carry):
@@ -345,7 +376,6 @@
         return carry
 
     lax.fori_loop(0, 4, to_z, 0)
-    finish_q(1)
 
     def back_slot(out, hh, ysrc):
         return out.at[0, :, pl.ds(m128(ysrc * GW + hh * HD), HD)]
@@ -380,27 +410,28 @@
         remote(part.at[xhd, xld], pin.at[n], ss10.at[n], rs10.at[n], dev(z, xld, c, y, xhd)).start()
     finish_q(2)
 
-    own = z * 2 + xh
     acc = part[xh, xl].astype(F32)
     for n in (1, 2, 3):
         landed(pin.at[n], rs10.at[n])
         acc = acc + pin[n].astype(F32)
-    redb[...] = acc.astype(BF16)
-    for n in range(8):
+    gst[y, xh] = acc.astype(BF16)
+    for n in range(1, 8):
         d, e = n // 2, n % 2
-        yd, xd = (y + d) % 4, (xh + e) % 2
-
-        def out_remote():
-            remote(redb, gwb.at[own], ss6.at[n], rs6.at[own], dev(y, xl, c, yd, xd)).start()
-
-        if n == 0:
-            pl.when(z != y)(out_remote)
-
-            @pl.when(z == y)
-            def _():
-                local_copy(redb, gwb.at[own], rs6.at[own]).start()
-        else:
-            out_remote()
+        remote(gst.at[y, xh], gst.at[y, xh], ss6.at[n], rs6.at[n], dev(z, xl, c, (y + d) % 4, (xh + e) % 2)).start()
+    for n in range(1, 8):
+        d, e = n // 2, n % 2
+        landed(gst.at[(y + 4 - d) % 4, (xh + e) % 2], rs6.at[n])
+
+    def gw_cols(zs, e):
+        return gw_out.at[:, pl.ds(m128((zs * 2 + e) * GW), GW)]
+
+    for d in (1, 2, 3):
+        zd = (z + d) % 4
+        for e in range(2):
+            n = (d - 1) * 2 + e
+            remote(gst.at[zd, e], gw_cols(z, e), ss13.at[n], rs13.at[n], dev(zd, xl, c, y, xh)).start()
+    for e in range(2):
+        local_copy(gst.at[z, e], gw_cols(z, e), lsw.at[e]).start()
 
     landed(q_cols(y), ls7.at[0])
     for d in (1, 2, 3):
@@ -416,9 +447,10 @@
         return carry
 
     lax.fori_loop(0, 3, collect, 0)
-    for n in range(8):
-        landed(gwb.at[n], rs6.at[n])
-        gw_out[:, n * GW : (n + 1) * GW] = gwb[n].astype(F32)
+    for e in range(2):
+        landed(gw_cols(z, e), lsw.at[e])
+        for d in (1, 2, 3):
+            landed(gw_cols((z + 4 - d) % 4, e), rs13.at[(d - 1) * 2 + e])
 
     @pl.when(z == y)
     def _():
@@ -451,14 +483,12 @@
     for n in range(3):
         landed(finq.at[n], ss7.at[n])
         landed(zin.at[n], ss11.at[n])
-        landed(redb, ss10.at[n + 1])
-
-    @pl.when(z != y)
-    def _():
-        landed(redb, ss6.at[0])
+        landed(pin.at[0], ss10.at[n + 1])
 
     for n in range(1, 8):
-        landed(redb, ss6.at[n])
+        landed(pin.at[0], ss6.at[n])
+    for n in range(6):
+        landed(pin.at[0], ss13.at[n])
 
 
 def local(query_rows, key_rows, value_rows, grad_out, w_out):
@@ -466,11 +496,11 @@
     dma = pltpu.SemaphoreType.DMA
     vm = pltpu.VMEM
     rows = jax.ShapeDtypeStruct((1, TOK, HW), BF16)
-    return pl.pallas_call(
+    gq, gk, gv, gw = pl.pallas_call(
         kernel,
-        out_shape=(rows, rows, rows, jax.ShapeDtypeStruct((96, D), F32)),
+        out_shape=(rows, rows, rows, jax.ShapeDtypeStruct((96, D), BF16)),
         in_specs=[any_spec] * 5,
-        out_specs=(any_spec, any_spec, any_spec, pl.BlockSpec(memory_space=pltpu.VMEM)),
+        out_specs=(any_spec,) * 4,
         scratch_shapes=[
             vm((3, 2 * HALF, HD), BF16),
             vm((3, HALF, HD), BF16),
@@ -508,8 +538,8 @@
             vm((3, 2, 2, 96, GW), BF16),
             vm((2, 2, 96, GW), BF16),
             vm((4, 96, GW), BF16),
-            vm((96, GW), BF16),
-            vm((8, 96, GW), BF16),
+            vm((4, 2, 96, GW), BF16),
+            vm((8, GW, GW), F32),
             dma((27,)), dma((27,)), dma((9,)),
             dma((3,)), dma((3,)),
             dma((6,)), dma((6,)), dma((1,)),
@@ -523,11 +553,13 @@
             dma((4,)), dma((4,)),
             dma((3,)), dma((3,)),
             dma((4,)), dma((4,)),
+            dma((6,)), dma((6,)), dma((2,)),
         ],
         compiler_params=pltpu.CompilerParams(
-            has_side_effects=True, vmem_limit_bytes=60 * 1024 * 1024
+            has_side_effects=True, collective_id=0, vmem_limit_bytes=60 * 1024 * 1024
         ),
     )(query_rows, key_rows, value_rows, grad_out, w_out)
+    return gq, gk, gv, gw.astype(F32)
 
 
 def solution(mesh):

time: 158 us -> 155 us (0.981)
  local copies, waits for them, and re-layouts: 6.12 us -> 2.65 us
  Pallas kernels: 151 us -> 148 us
  other arithmetic: 0 us -> 2.29 us
    unnamed x10 -> x9, local copies, waits for them, and re-layouts: 6.12 us -> 2.65 us
    pallas_call x1, Pallas kernels: 151 us -> 148 us  [local(): pl.pallas_call(kernel, out_shape=(rows, rows, rows, jax.ShapeDtypeStruct(...]
    convert_element_type x0 -> x1, other arithmetic: none -> 2.29 us  [local(): return (gq, gk, gv, gw.astype(F32))]
where the time goes in v4:
time: 155 us; the launch traced here: 154 us
  Pallas kernels  148 us (95%)
  local copies, waits for them, and re-layouts  2.65 us (2%)
  other arithmetic  2.29 us (1%)
    pallas_call x1, Pallas kernels, local(): pl.pallas_call(kernel, out_shape=(rows, rows, rows, jax.ShapeDtypeStruct(...  148 us

profile of v4, /device:TPU:16, one launch (start us, length us, event | category | flops | bytes accessed | tf_op | source)
XLA Modules:
  0.0 153.5 jit_solution(1058438444583508675)
XLA Ops:
  0.6 147.9 %shard_map.84 = (bf16[1,256,1536]{2,1,0:T(8,128)(2,1)}, bf16[1,256,1536]{2,1,0:T(8,128)(2,1)}, bf16[1,256,1536]{2,1,0:T(8,128)(2,1)}, bf16[96,3072]{1,0:T(8,128)(2,1)}) custom-call(bf16[1,256,1536]{2,1,0:T(8,128)(2,1)} %q_hbm.1, bf16[1,256,1536]{2,1,0:T(8,128)(2,1)} %k_hbm.1, bf16[1,256,1536]{2,1,0:T(8,128)(2,1)} %v_hbm.1, bf16[1,256,3072]{2,1,0:T(8,128)(2,1)} %go_hbm.1, ...), custom_call_target="tpu_custom_call" | custom-call | tf_op jit(solution)/shard_map/pallas_call | solution.py:499
  148.5 0.0 copy-start.2
  148.6 0.0 copy-start.1
  148.6 2.3 %convert_element_type.3 = f32[96,3072]{1,0:T(8,128)} convert(bf16[96,3072]{1,0:T(8,128)(2,1)} %get-tuple-element.11) | non-fusion elementwise | flops 294912 | bytes 1769472 | tf_op jit(solution)/shard_map/convert_element_type | solution.py:562
  150.9 0.0 copy-done.2
  150.9 0.0 copy-start
  150.9 0.9 copy.12
  151.7 0.0 copy-done.1
  151.7 0.9 copy.13
  152.6 0.0 copy-done
  152.6 0.9 copy.14
Async XLA Ops:
  148.5 2.3 %copy-start.2 = (bf16[1,256,1536]{2,1,0:T(8,128)(2,1)S(1)}, bf16[1,256,1536]{2,1,0:T(8,128)(2,1)}, u32[]{:S(2)}) copy-start(bf16[1,256,1536]{2,1,0:T(8,128)(2,1)} %get-tuple-element.16) | copy-start | bytes 2359300
  148.6 3.2 %copy-start.1 = (bf16[1,256,1536]{2,1,0:T(8,128)(2,1)S(1)}, bf16[1,256,1536]{2,1,0:T(8,128)(2,1)}, u32[]{:S(2)}) copy-start(bf16[1,256,1536]{2,1,0:T(8,128)(2,1)} %get-tuple-element.17) | copy-start | bytes 2359300
  150.9 1.8 %copy-start = (bf16[1,256,1536]{2,1,0:T(8,128)(2,1)S(1)}, bf16[1,256,1536]{2,1,0:T(8,128)(2,1)}, u32[]{:S(2)}) copy-start(bf16[1,256,1536]{2,1,0:T(8,128)(2,1)} %get-tuple-element.18) | copy-start | bytes 2359300

commit v5 on v4

--- a/solution.py
+++ b/solution.py
@@ -54,10 +54,10 @@
     gq_out, gk_out, gv_out, gw_out,
     qbuf, kbuf, vbuf, ktb, vtb, go, wbuf, sbuf, pbuf, att, obuf, stat, rbuf,
     oxs, oxr, sxs, sxr, g1, c1, gxs, gxr, cxs, cxr, dqk, dqxs, dqxr, finq,
-    dkacc, dvacc, fin, termb, cin, zsum, zin, part, pin, gst, tacc,
+    dkacc, dvacc, fin, termb, cin, zsum, zin, part, pin, redb, tacc,
     ss1, rs1, ls1, ss2, rs2, ss3, rs3, lsg, ssw1, rsw1, ssw2, rsw2,
     ss4, rs4, ss5, rs5, ss6, rs6, ss7, rs7, ls7, ss8, rs8, ss9, rs9, ls9,
-    ss10, rs10, ss11, rs11, ss12, rs12, ss13, rs13, lsw,
+    ss10, rs10, ss11, rs11, ss12, rs12,
 ):
     f = lax.axis_index("fsdp")
     r = lax.axis_index("rows")
@@ -361,22 +361,6 @@
     finish_q(1)
     backward(True, yo)
 
-    def to_z(o, carry):
-        zd = (z + 1 + o) % 4
-        landed(cin.at[zd], rs5.at[zd])
-        for e in range(2):
-            for a in range(2):
-                t = termb[zd, c, e, a].astype(F32) + cin[zd, e, a].astype(F32)
-                zsum[o, e, a] = t.astype(BF16)
-
-        @pl.when(o < 3)
-        def _():
-            remote(zsum.at[o], zin.at[o], ss11.at[o], rs11.at[o], dev(zd, xl, c, y, xh)).start()
-
-        return carry
-
-    lax.fori_loop(0, 4, to_z, 0)
-
     def back_slot(out, hh, ysrc):
         return out.at[0, :, pl.ds(m128(ysrc * GW + hh * HD), HD)]
 
@@ -395,6 +379,22 @@
     theirs_in(yo)
     backward(False, yo, hand_out)
     send_dq(yo)
+
+    def to_z(o, carry):
+        zd = (z + 1 + o) % 4
+        landed(cin.at[zd], rs5.at[zd])
+        for e in range(2):
+            for a in range(2):
+                t = termb[zd, c, e, a].astype(F32) + cin[zd, e, a].astype(F32)
+                zsum[o, e, a] = t.astype(BF16)
+
+        @pl.when(o < 3)
+        def _():
+            remote(zsum.at[o], zin.at[o], ss11.at[o], rs11.at[o], dev(zd, xl, c, y, xh)).start()
+
+        return carry
+
+    lax.fori_loop(0, 4, to_z, 0)
 
     for i in range(3):
         landed(zin.at[i], rs11.at[i])
@@ -414,24 +414,27 @@
     for n in (1, 2, 3):
         landed(pin.at[n], rs10.at[n])
         acc = acc + pin[n].astype(F32)
-    gst[y, xh] = acc.astype(BF16)
-    for n in range(1, 8):
-        d, e = n // 2, n % 2
-        remote(gst.at[y, xh], gst.at[y, xh], ss6.at[n], rs6.at[n], dev(z, xl, c, (y + d) % 4, (xh + e) % 2)).start()
-    for n in range(1, 8):
-        d, e = n // 2, n % 2
-        landed(gst.at[(y + 4 - d) % 4, (xh + e) % 2], rs6.at[n])
+    redb[...] = acc.astype(BF16)
 
     def gw_cols(zs, e):
         return gw_out.at[:, pl.ds(m128((zs * 2 + e) * GW), GW)]
 
-    for d in (1, 2, 3):
-        zd = (z + d) % 4
-        for e in range(2):
-            n = (d - 1) * 2 + e
-            remote(gst.at[zd, e], gw_cols(z, e), ss13.at[n], rs13.at[n], dev(zd, xl, c, y, xh)).start()
-    for e in range(2):
-        local_copy(gst.at[z, e], gw_cols(z, e), lsw.at[e]).start()
+    own = z * 2 + xh
+    for n in range(8):
+        d, e = n // 2, n % 2
+        yd, xd = (y + d) % 4, (xh + e) % 2
+
+        def to_owner():
+            remote(redb, gw_cols(z, xh), ss6.at[n], rs6.at[own], dev(y, xl, c, yd, xd)).start()
+
+        if n == 0:
+            pl.when(z != y)(to_owner)
+
+            @pl.when(z == y)
+            def _():
+                local_copy(redb, gw_cols(z, xh), rs6.at[own]).start()
+        else:
+            to_owner()
 
     landed(q_cols(y), ls7.at[0])
     for d in (1, 2, 3):
@@ -447,10 +450,8 @@
         return carry
 
     lax.fori_loop(0, 3, collect, 0)
-    for e in range(2):
-        landed(gw_cols(z, e), lsw.at[e])
-        for d in (1, 2, 3):
-            landed(gw_cols((z + 4 - d) % 4, e), rs13.at[(d - 1) * 2 + e])
+    for n in range(8):
+        landed(gw_cols(n // 2, n % 2), rs6.at[n])
 
     @pl.when(z == y)
     def _():
@@ -485,10 +486,19 @@
         landed(zin.at[n], ss11.at[n])
         landed(pin.at[0], ss10.at[n + 1])
 
+    @pl.when(z != y)
+    def _():
+        landed(redb, ss6.at[0])
+
     for n in range(1, 8):
-        landed(pin.at[0], ss6.at[n])
-    for n in range(6):
-        landed(pin.at[0], ss13.at[n])
+        landed(redb, ss6.at[n])
+
+
+def store(gq, gk, gv, gw, gq_out, gk_out, gv_out, gw_out):
+    gq_out[...] = gq[...]
+    gk_out[...] = gk[...]
+    gv_out[...] = gv[...]
+    gw_out[...] = gw[...].astype(F32)
 
 
 def local(query_rows, key_rows, value_rows, grad_out, w_out):
@@ -538,7 +548,7 @@
             vm((3, 2, 2, 96, GW), BF16),
             vm((2, 2, 96, GW), BF16),
             vm((4, 96, GW), BF16),
-            vm((4, 2, 96, GW), BF16),
+            vm((96, GW), BF16),
             vm((8, GW, GW), F32),
             dma((27,)), dma((27,)), dma((9,)),
             dma((3,)), dma((3,)),
@@ -553,13 +563,20 @@
             dma((4,)), dma((4,)),
             dma((3,)), dma((3,)),
             dma((4,)), dma((4,)),
-            dma((6,)), dma((6,)), dma((2,)),
         ],
         compiler_params=pltpu.CompilerParams(
             has_side_effects=True, collective_id=0, vmem_limit_bytes=60 * 1024 * 1024
         ),
     )(query_rows, key_rows, value_rows, grad_out, w_out)
-    return gq, gk, gv, gw.astype(F32)
+    half = pl.BlockSpec((1, TOK // 2, HW), lambda i: (0, i, 0))
+    part = pl.BlockSpec((48, D), lambda i: (i, 0))
+    return pl.pallas_call(
+        store,
+        out_shape=(rows, rows, rows, jax.ShapeDtypeStruct((96, D), F32)),
+        grid=(2,),
+        in_specs=[half] * 3 + [part],
+        out_specs=[half] * 3 + [part],
+    )(gq, gk, gv, gw)
 
 
 def solution(mesh):

time: 155 us -> 147 us (0.948); the launches traced: 154 us -> 147 us
  local copies, waits for them, and re-layouts: 2.65 us -> 0 us
  other arithmetic: 2.29 us -> 0 us
  Pallas kernels: 148 us -> 146 us
    pallas_call x1, Pallas kernels: 148 us -> 143 us  [local(): pl.pallas_call(kernel, out_shape=(rows, rows, rows, jax.ShapeDtypeStruct(...]
    pallas_call x0 -> x1, Pallas kernels: none -> 3.22 us  [local(): pl.pallas_call(store, out_shape=(rows, rows, rows, jax.ShapeDtypeStruct((...]
    unnamed x9 -> x0, local copies, waits for them, and re-layouts: 2.65 us -> none
    convert_element_type x1 -> x0, other arithmetic: 2.29 us -> none  [local(): return (gq, gk, gv, gw.astype(F32))]
where the time goes in v5:
time: 147 us
  Pallas kernels  146 us (99%)
    pallas_call x1, Pallas kernels, local(): pl.pallas_call(kernel, out_shape=(rows, rows, rows, jax.ShapeDtypeStruct(...  143 us
    pallas_call x1, Pallas kernels, local(): pl.pallas_call(store, out_shape=(rows, rows, rows, jax.ShapeDtypeStruct((...  3.22 us

profile of v5, /device:TPU:16, one launch (start us, length us, event | category | flops | bytes accessed | tf_op | source)
XLA Modules:
  0.0 147.1 jit_solution(1871184489078892115)
XLA Ops:
  0.6 143.2 %shard_map.84 = (bf16[1,256,1536]{2,1,0:T(8,128)(2,1)}, bf16[1,256,1536]{2,1,0:T(8,128)(2,1)}, bf16[1,256,1536]{2,1,0:T(8,128)(2,1)}, bf16[96,3072]{1,0:T(8,128)(2,1)}) custom-call(bf16[1,256,1536]{2,1,0:T(8,128)(2,1)} %q_hbm.1, bf16[1,256,1536]{2,1,0:T(8,128)(2,1)} %k_hbm.1, bf16[1,256,1536]{2,1,0:T(8,128)(2,1)} %v_hbm.1, bf16[1,256,3072]{2,1,0:T(8,128)(2,1)} %go_hbm.1, ...), custom_call_target="tpu_custom_call" | custom-call | tf_op jit(solution)/shard_map/pallas_call | solution.py:509
  143.9 3.2 %shard_map.85 = (bf16[1,256,1536]{2,1,0:T(8,128)(2,1)}, bf16[1,256,1536]{2,1,0:T(8,128)(2,1)}, bf16[1,256,1536]{2,1,0:T(8,128)(2,1)}, f32[96,3072]{1,0:T(8,128)}) custom-call(bf16[1,256,1536]{2,1,0:T(8,128)(2,1)} %get-tuple-element.8.gq, bf16[1,256,1536]{2,1,0:T(8,128)(2,1)} %get-tuple-element.9.gk, bf16[1,256,1536]{2,1,0:T(8,128)(2,1)} %get-tuple-element.10.gv, ...), custom_call_target="tpu_custom_call" | custom-call | tf_op jit(solution)/shard_map/pallas_call | solution.py:573

commit v6 on v5

--- a/solution.py
+++ b/solution.py
@@ -54,10 +54,10 @@
     gq_out, gk_out, gv_out, gw_out,
     qbuf, kbuf, vbuf, ktb, vtb, go, wbuf, sbuf, pbuf, att, obuf, stat, rbuf,
     oxs, oxr, sxs, sxr, g1, c1, gxs, gxr, cxs, cxr, dqk, dqxs, dqxr, finq,
-    dkacc, dvacc, fin, termb, cin, zsum, zin, part, pin, redb, tacc,
+    dkacc, dvacc, fin, termb, cin, zsum, zin, xsum, xin, hsum, hin, part, pin, redb, tacc,
     ss1, rs1, ls1, ss2, rs2, ss3, rs3, lsg, ssw1, rsw1, ssw2, rsw2,
     ss4, rs4, ss5, rs5, ss6, rs6, ss7, rs7, ls7, ss8, rs8, ss9, rs9, ls9,
-    ss10, rs10, ss11, rs11, ss12, rs12,
+    ss10, rs10, ss11, rs11, ss12, rs12, ss13, rs13, ss14, rs14,
 ):
     f = lax.axis_index("fsdp")
     r = lax.axis_index("rows")
@@ -243,45 +243,51 @@
             gxs[ys, hh] = (gh * rb).astype(BF16)
             c1[ys, hh, 0:1, :] = cen * ra
             cxs[ys, hh, 0:1, :] = cen * rb
-        remote(gxs.at[ys], gxr.at[ys], ss8.at[ys], rs8.at[ys], partner).start()
-        remote(cxs.at[ys], cxr.at[ys], ss8.at[ys + 4], rs8.at[ys + 4], partner).start()
+            i = ys * 3 + hh
+            remote(gxs.at[ys, hh], gxr.at[ys, hh], ss8.at[i], rs8.at[i], partner).start()
+            remote(cxs.at[ys, hh], cxr.at[ys, hh], ss8.at[i + 12], rs8.at[i + 12], partner).start()
 
     dkacc[...] = jnp.zeros_like(dkacc)
     dvacc[...] = jnp.zeros_like(dvacc)
 
-    def backward(own, ys, after=None):
+    def one_head(own, ys, hh):
         s = (xh if own else 1 - xh) * 4 + ys
-
+        i = hh * 8 + s
+        qn = qbuf[hh, pl.ds(m256(s * TOK), TOK), :]
+        gt = (g1 if own else gxr)[ys, hh]
+        cen = (c1 if own else cxr)[ys, hh, 0:1, :]
+        gn = gt.T
+        dq = jnp.zeros((HD, TOK), F32)
+        for kc in range(NK):
+            ks = slice(kc * KC, (kc + 1) * KC)
+            dp = dot(vbuf[hh, ks, :], gt)
+            pb = pbuf[i, ks, :]
+            ds = (pb.astype(F32) * (dp - cen)).astype(BF16)
+            dq = dq + dot(ktb[hh, :, ks], ds)
+            dkacc[hh, ks, :] += dot(ds, qn)
+            dvacc[hh, ks, :] += dot(pb, gn)
+        dqn = (dq * SCALE).T
+        hs = pl.ds(m128(hh * HD), HD)
+        if own:
+            dqk[ys, :, hs] = dqn
+        else:
+            dqxs[ys, :, hs] = dqn.astype(BF16)
+
+    def head_in(ys, hh):
+        i = ys * 3 + hh
+        landed(gxr.at[ys, hh], rs8.at[i])
+        landed(cxr.at[ys, hh], rs8.at[i + 12])
+
+    def backward(own, ys):
         def head(hh, carry):
-            i = hh * 8 + s
-            qn = qbuf[hh, pl.ds(m256(s * TOK), TOK), :]
-            gt = (g1 if own else gxr)[ys, hh]
-            cen = (c1 if own else cxr)[ys, hh, 0:1, :]
-            gn = gt.T
-            dq = jnp.zeros((HD, TOK), F32)
-            for kc in range(NK):
-                ks = slice(kc * KC, (kc + 1) * KC)
-                dp = dot(vbuf[hh, ks, :], gt)
-                pb = pbuf[i, ks, :]
-                ds = (pb.astype(F32) * (dp - cen)).astype(BF16)
-                dq = dq + dot(ktb[hh, :, ks], ds)
-                dkacc[hh, ks, :] += dot(ds, qn)
-                dvacc[hh, ks, :] += dot(pb, gn)
-            dqn = (dq * SCALE).T
-            hs = pl.ds(m128(hh * HD), HD)
-            if own:
-                dqk[ys, :, hs] = dqn
-            else:
-                dqxs[ys, :, hs] = dqn.astype(BF16)
-            if after is not None:
-                after(hh)
+            one_head(own, ys, hh)
             return carry
 
         lax.fori_loop(0, 3, head, 0)
 
     def theirs_in(ys):
-        landed(gxr.at[ys], rs8.at[ys])
-        landed(cxr.at[ys], rs8.at[ys + 4])
+        for hh in range(3):
+            head_in(ys, hh)
 
     def send_dq(ys):
         remote(dqxs.at[ys], dqxr.at[ys], ss12.at[ys], rs12.at[ys], partner).start()
@@ -342,6 +348,8 @@
     term_part(yl)
     term_part(yr)
     finish_q(0)
+    finish_q(3)
+    finish_q(1)
 
     landed(go_slot(yo, 0), rs3.at[4])
     landed(go_slot(yo, 1), rs3.at[5])
@@ -357,9 +365,6 @@
         return carry
 
     lax.fori_loop(0, 4, term, 0)
-    finish_q(3)
-    finish_q(1)
-    backward(True, yo)
 
     def back_slot(out, hh, ysrc):
         return out.at[0, :, pl.ds(m128(ysrc * GW + hh * HD), HD)]
@@ -376,17 +381,16 @@
                        ydev(yd)).start()
             local_copy(fin.at[i, pl.ds(m256(y * TOK), TOK), :], back_slot(out, hh, y), ls9.at[i]).start()
 
-    theirs_in(yo)
-    backward(False, yo, hand_out)
-    send_dq(yo)
-
-    def to_z(o, carry):
+    backward(True, yo)
+
+    def to_mates(o, carry):
         zd = (z + 1 + o) % 4
         landed(cin.at[zd], rs5.at[zd])
         for e in range(2):
             for a in range(2):
-                t = termb[zd, c, e, a].astype(F32) + cin[zd, e, a].astype(F32)
-                zsum[o, e, a] = t.astype(BF16)
+                t = (termb[zd, c, e, a].astype(F32) + cin[zd, e, a].astype(F32)).astype(BF16)
+                zsum[o, e, a] = t[:48, :]
+                xsum[e, a, zd] = t[48:, :]
 
         @pl.when(o < 3)
         def _():
@@ -394,8 +398,30 @@
 
         return carry
 
-    lax.fori_loop(0, 4, to_z, 0)
-
+    lax.fori_loop(0, 4, to_mates, 0)
+    x_mates = [(n, (xl + n // 2) % 2, (xh + n % 2) % 2) for n in (1, 2, 3)]
+    for n, xld, xhd in x_mates:
+        remote(xsum.at[xhd, xld], xin.at[n], ss13.at[n], rs13.at[n], dev(z, xld, c, y, xhd)).start()
+
+    def last_head(hh, carry):
+        head_in(yo, hh)
+        one_head(False, yo, hh)
+        hand_out(hh)
+        return carry
+
+    lax.fori_loop(0, 3, last_head, 0)
+    send_dq(yo)
+
+    for n in (1, 2, 3):
+        landed(xin.at[n], rs13.at[n])
+    for zd in range(4):
+        t = xsum[xh, xl, zd].astype(F32)
+        for n in (1, 2, 3):
+            t = t + xin[n, zd].astype(F32)
+        hsum[zd] = t.astype(BF16)
+    for d in (1, 2, 3):
+        zd = (z + d) % 4
+        remote(hsum.at[zd], hin.at[d], ss14.at[d], rs14.at[d], dev(zd, xl, c, y, xh)).start()
     for i in range(3):
         landed(zin.at[i], rs11.at[i])
     for e in range(2):
@@ -404,17 +430,19 @@
             for i in range(3):
                 t = t + zin[i, e, a].astype(F32)
             part[e, a] = t.astype(BF16)
-    for n in (1, 2, 3):
-        a, e = n // 2, n % 2
-        xld, xhd = (xl + a) % 2, (xh + e) % 2
+    for n, xld, xhd in x_mates:
         remote(part.at[xhd, xld], pin.at[n], ss10.at[n], rs10.at[n], dev(z, xld, c, y, xhd)).start()
     finish_q(2)
 
-    acc = part[xh, xl].astype(F32)
+    upper, lower = part[xh, xl].astype(F32), hsum[z].astype(F32)
+    for n in (1, 2, 3):
+        landed(hin.at[n], rs14.at[n])
+        lower = lower + hin[n].astype(F32)
     for n in (1, 2, 3):
         landed(pin.at[n], rs10.at[n])
-        acc = acc + pin[n].astype(F32)
-    redb[...] = acc.astype(BF16)
+        upper = upper + pin[n].astype(F32)
+    redb[:48, :] = upper.astype(BF16)
+    redb[48:, :] = lower.astype(BF16)
 
     def gw_cols(zs, e):
         return gw_out.at[:, pl.ds(m128((zs * 2 + e) * GW), GW)]
@@ -477,14 +505,17 @@
     for n in range(6):
         landed(go_slot(y, 0), ss3.at[n])
     for n in range(4):
-        landed(gxs.at[n], ss8.at[n])
-        landed(cxs.at[n], ss8.at[n + 4])
+        for hh in range(3):
+            landed(gxs.at[n, hh], ss8.at[n * 3 + hh])
+            landed(cxs.at[n, hh], ss8.at[n * 3 + hh + 12])
         landed(dqxs.at[n], ss12.at[n])
         landed(cin.at[n], ss5.at[n])
     for n in range(3):
         landed(finq.at[n], ss7.at[n])
         landed(zin.at[n], ss11.at[n])
         landed(pin.at[0], ss10.at[n + 1])
+        landed(xin.at[0], ss13.at[n + 1])
+        landed(hin.at[0], ss14.at[n + 1])
 
     @pl.when(z != y)
     def _():
@@ -544,10 +575,14 @@
             vm((6, HALF, HD), BF16),
             vm((4, 2, 2, 2, 96, GW), BF16),
             vm((4, 2, 2, 96, GW), BF16),
-            vm((4, 2, 2, 96, GW), BF16),
-            vm((3, 2, 2, 96, GW), BF16),
-            vm((2, 2, 96, GW), BF16),
-            vm((4, 96, GW), BF16),
+            vm((4, 2, 2, 48, GW), BF16),
+            vm((3, 2, 2, 48, GW), BF16),
+            vm((2, 2, 4, 48, GW), BF16),
+            vm((4, 4, 48, GW), BF16),
+            vm((4, 48, GW), BF16),
+            vm((4, 48, GW), BF16),
+            vm((2, 2, 48, GW), BF16),
+            vm((4, 48, GW), BF16),
             vm((96, GW), BF16),
             vm((8, GW, GW), F32),
             dma((27,)), dma((27,)), dma((9,)),
@@ -558,11 +593,12 @@
             dma((4,)), dma((4,)),
             dma((8,)), dma((8,)),
             dma((3,)), dma((3,)), dma((1,)),
-            dma((8,)), dma((8,)),
+            dma((24,)), dma((24,)),
             dma((18,)), dma((18,)), dma((6,)),
             dma((4,)), dma((4,)),
             dma((3,)), dma((3,)),
             dma((4,)), dma((4,)),
+            dma((4,)), dma((4,)), dma((4,)), dma((4,)),
         ],
         compiler_params=pltpu.CompilerParams(
             has_side_effects=True, collective_id=0, vmem_limit_bytes=60 * 1024 * 1024

time: 147 us -> 149 us (1.014)
  Pallas kernels: 146 us -> 148 us
where the time goes in v6:
time: 149 us; the launch traced here: 148 us
  Pallas kernels  148 us (99%)
    pallas_call x1, Pallas kernels, local(): pl.pallas_call(kernel, out_shape=(rows, rows, rows, jax.ShapeDtypeStruct(...  145 us
    pallas_call x1, Pallas kernels, local(): pl.pallas_call(store, out_shape=(rows, rows, rows, jax.ShapeDtypeStruct((...  3.22 us

profile of v6, /device:TPU:16, one launch (start us, length us, event | category | flops | bytes accessed | tf_op | source)
XLA Modules:
  0.0 148.4 jit_solution(4584063044054860957)
XLA Ops:
  0.6 144.5 %shard_map.84 = (bf16[1,256,1536]{2,1,0:T(8,128)(2,1)}, bf16[1,256,1536]{2,1,0:T(8,128)(2,1)}, bf16[1,256,1536]{2,1,0:T(8,128)(2,1)}, bf16[96,3072]{1,0:T(8,128)(2,1)}) custom-call(bf16[1,256,1536]{2,1,0:T(8,128)(2,1)} %q_hbm.1, bf16[1,256,1536]{2,1,0:T(8,128)(2,1)} %k_hbm.1, bf16[1,256,1536]{2,1,0:T(8,128)(2,1)} %v_hbm.1, bf16[1,256,3072]{2,1,0:T(8,128)(2,1)} %go_hbm.1, ...), custom_call_target="tpu_custom_call" | custom-call | tf_op jit(solution)/shard_map/pallas_call | solution.py:540
  145.2 3.2 %shard_map.85 = (bf16[1,256,1536]{2,1,0:T(8,128)(2,1)}, bf16[1,256,1536]{2,1,0:T(8,128)(2,1)}, bf16[1,256,1536]{2,1,0:T(8,128)(2,1)}, f32[96,3072]{1,0:T(8,128)}) custom-call(bf16[1,256,1536]{2,1,0:T(8,128)(2,1)} %get-tuple-element.8.gq, bf16[1,256,1536]{2,1,0:T(8,128)(2,1)} %get-tuple-element.9.gk, bf16[1,256,1536]{2,1,0:T(8,128)(2,1)} %get-tuple-element.10.gv, ...), custom_call_target="tpu_custom_call" | custom-call | tf_op jit(solution)/shard_map/pallas_call | solution.py:609

commit v7 on v6

--- a/solution.py
+++ b/solution.py
@@ -54,10 +54,10 @@
     gq_out, gk_out, gv_out, gw_out,
     qbuf, kbuf, vbuf, ktb, vtb, go, wbuf, sbuf, pbuf, att, obuf, stat, rbuf,
     oxs, oxr, sxs, sxr, g1, c1, gxs, gxr, cxs, cxr, dqk, dqxs, dqxr, finq,
-    dkacc, dvacc, fin, termb, cin, zsum, zin, xsum, xin, hsum, hin, part, pin, redb, tacc,
+    dkacc, dvacc, fin, termb, cin, zsum, zin, part, pin, redb, tacc,
     ss1, rs1, ls1, ss2, rs2, ss3, rs3, lsg, ssw1, rsw1, ssw2, rsw2,
     ss4, rs4, ss5, rs5, ss6, rs6, ss7, rs7, ls7, ss8, rs8, ss9, rs9, ls9,
-    ss10, rs10, ss11, rs11, ss12, rs12, ss13, rs13, ss14, rs14,
+    ss10, rs10, ss11, rs11, ss12, rs12,
 ):
     f = lax.axis_index("fsdp")
     r = lax.axis_index("rows")
@@ -383,14 +383,13 @@
 
     backward(True, yo)
 
-    def to_mates(o, carry):
+    def to_z(o, carry):
         zd = (z + 1 + o) % 4
         landed(cin.at[zd], rs5.at[zd])
         for e in range(2):
             for a in range(2):
-                t = (termb[zd, c, e, a].astype(F32) + cin[zd, e, a].astype(F32)).astype(BF16)
-                zsum[o, e, a] = t[:48, :]
-                xsum[e, a, zd] = t[48:, :]
+                t = termb[zd, c, e, a].astype(F32) + cin[zd, e, a].astype(F32)
+                zsum[o, e, a] = t.astype(BF16)
 
         @pl.when(o < 3)
         def _():
@@ -398,10 +397,8 @@
 
         return carry
 
-    lax.fori_loop(0, 4, to_mates, 0)
-    x_mates = [(n, (xl + n // 2) % 2, (xh + n % 2) % 2) for n in (1, 2, 3)]
-    for n, xld, xhd in x_mates:
-        remote(xsum.at[xhd, xld], xin.at[n], ss13.at[n], rs13.at[n], dev(z, xld, c, y, xhd)).start()
+    lax.fori_loop(0, 4, to_z, 0)
+
 
     def last_head(hh, carry):
         head_in(yo, hh)
@@ -412,16 +409,6 @@
     lax.fori_loop(0, 3, last_head, 0)
     send_dq(yo)
 
-    for n in (1, 2, 3):
-        landed(xin.at[n], rs13.at[n])
-    for zd in range(4):
-        t = xsum[xh, xl, zd].astype(F32)
-        for n in (1, 2, 3):
-            t = t + xin[n, zd].astype(F32)
-        hsum[zd] = t.astype(BF16)
-    for d in (1, 2, 3):
-        zd = (z + d) % 4
-        remote(hsum.at[zd], hin.at[d], ss14.at[d], rs14.at[d], dev(zd, xl, c, y, xh)).start()
     for i in range(3):
         landed(zin.at[i], rs11.at[i])
     for e in range(2):
@@ -430,19 +417,17 @@
             for i in range(3):
                 t = t + zin[i, e, a].astype(F32)
             part[e, a] = t.astype(BF16)
-    for n, xld, xhd in x_mates:
+    for n in (1, 2, 3):
+        a, e = n // 2, n % 2
+        xld, xhd = (xl + a) % 2, (xh + e) % 2
         remote(part.at[xhd, xld], pin.at[n], ss10.at[n], rs10.at[n], dev(z, xld, c, y, xhd)).start()
     finish_q(2)
 
-    upper, lower = part[xh, xl].astype(F32), hsum[z].astype(F32)
-    for n in (1, 2, 3):
-        landed(hin.at[n], rs14.at[n])
-        lower = lower + hin[n].astype(F32)
+    acc = part[xh, xl].astype(F32)
     for n in (1, 2, 3):
         landed(pin.at[n], rs10.at[n])
-        upper = upper + pin[n].astype(F32)
-    redb[:48, :] = upper.astype(BF16)
-    redb[48:, :] = lower.astype(BF16)
+        acc = acc + pin[n].astype(F32)
+    redb[...] = acc.astype(BF16)
 
     def gw_cols(zs, e):
         return gw_out.at[:, pl.ds(m128((zs * 2 + e) * GW), GW)]
@@ -514,8 +499,6 @@
         landed(finq.at[n], ss7.at[n])
         landed(zin.at[n], ss11.at[n])
         landed(pin.at[0], ss10.at[n + 1])
-        landed(xin.at[0], ss13.at[n + 1])
-        landed(hin.at[0], ss14.at[n + 1])
 
     @pl.when(z != y)
     def _():
@@ -575,14 +558,10 @@
             vm((6, HALF, HD), BF16),
             vm((4, 2, 2, 2, 96, GW), BF16),
             vm((4, 2, 2, 96, GW), BF16),
-            vm((4, 2, 2, 48, GW), BF16),
-            vm((3, 2, 2, 48, GW), BF16),
-            vm((2, 2, 4, 48, GW), BF16),
-            vm((4, 4, 48, GW), BF16),
-            vm((4, 48, GW), BF16),
-            vm((4, 48, GW), BF16),
-            vm((2, 2, 48, GW), BF16),
-            vm((4, 48, GW), BF16),
+            vm((4, 2, 2, 96, GW), BF16),
+            vm((3, 2, 2, 96, GW), BF16),
+            vm((2, 2, 96, GW), BF16),
+            vm((4, 96, GW), BF16),
             vm((96, GW), BF16),
             vm((8, GW, GW), F32),
             dma((27,)), dma((27,)), dma((9,)),
@@ -598,7 +577,6 @@
             dma((4,)), dma((4,)),
             dma((3,)), dma((3,)),
             dma((4,)), dma((4,)),
-            dma((4,)), dma((4,)), dma((4,)), dma((4,)),
         ],
         compiler_params=pltpu.CompilerParams(
             has_side_effects=True, collective_id=0, vmem_limit_bytes=60 * 1024 * 1024

time: 149 us -> 148 us (level)
  no operation moved by 1% of the time
where the time goes in v7:
time: 148 us
  Pallas kernels  147 us (99%)
    pallas_call x1, Pallas kernels, local(): pl.pallas_call(kernel, out_shape=(rows, rows, rows, jax.ShapeDtypeStruct(...  144 us
    pallas_call x1, Pallas kernels, local(): pl.pallas_call(store, out_shape=(rows, rows, rows, jax.ShapeDtypeStruct((...  3.22 us

profile of v7, /device:TPU:16, one launch (start us, length us, event | category | flops | bytes accessed | tf_op | source)
XLA Modules:
  0.0 147.9 jit_solution(12617124766765687946)
XLA Ops:
  0.6 144.1 %shard_map.84 = (bf16[1,256,1536]{2,1,0:T(8,128)(2,1)}, bf16[1,256,1536]{2,1,0:T(8,128)(2,1)}, bf16[1,256,1536]{2,1,0:T(8,128)(2,1)}, bf16[96,3072]{1,0:T(8,128)(2,1)}) custom-call(bf16[1,256,1536]{2,1,0:T(8,128)(2,1)} %q_hbm.1, bf16[1,256,1536]{2,1,0:T(8,128)(2,1)} %k_hbm.1, bf16[1,256,1536]{2,1,0:T(8,128)(2,1)} %v_hbm.1, bf16[1,256,3072]{2,1,0:T(8,128)(2,1)} %go_hbm.1, ...), custom_call_target="tpu_custom_call" | custom-call | tf_op jit(solution)/shard_map/pallas_call | solution.py:523
  144.7 3.2 %shard_map.85 = (bf16[1,256,1536]{2,1,0:T(8,128)(2,1)}, bf16[1,256,1536]{2,1,0:T(8,128)(2,1)}, bf16[1,256,1536]{2,1,0:T(8,128)(2,1)}, f32[96,3072]{1,0:T(8,128)}) custom-call(bf16[1,256,1536]{2,1,0:T(8,128)(2,1)} %get-tuple-element.8.gq, bf16[1,256,1536]{2,1,0:T(8,128)(2,1)} %get-tuple-element.9.gk, bf16[1,256,1536]{2,1,0:T(8,128)(2,1)} %get-tuple-element.10.gv, ...), custom_call_target="tpu_custom_call" | custom-call | tf_op jit(solution)/shard_map/pallas_call | solution.py:587
